TPU v7x, 32 devices: a whole 2x2x4 slice. The times are simulated.
32 devices in a mesh: row: 8 (over y, x, core), col: 4 (over z).
Axes of the slice: x: 2, y: 2, z: 4, core: 2. Of those that a mesh axis runs over, the one named last changes fastest.
Arguments:
- matrix: bfloat16 [16384, 8192], P('row', 'col'), may hold values from 0 to 1
- labels: int32 [16384, 1], P('row'), may hold values from 0 to 7
- root_rows: float32 [8, 16384], P(None, 'row'), may hold values from 0.2 to 1
- root_cols: float32 [8, 8192], P(None, 'col'), may hold values from 0.2 to 1
- child_rows: float32 [16, 16384], P(None, 'row'), may hold values from 0.2 to 1
- child_cols: float32 [128, 8192], P(None, 'col'), may hold values from 0.2 to 1
Outputs:
- root_w: float32 [8, 16384], P(None, 'row')
- root_h: float32 [8, 8192], P(None, 'col')
- child_w: float32 [16, 16384], P(None, 'row')
- child_h: float32 [128, 8192], P(None, 'col')
Inputs may be any that keep to these rules, and one draw needn't show every extreme that they name: `labels`: every cluster 0 to 7 holds at least one node.
All inputs are finite; a program needn't handle non-finite values.
Results may differ from a plain program's by a relative error of at most 0.00035.
Values sent between devices are 32-bit elements; how exact they have to be, the bound alone decides.
No kernel may reach another device: no remote copies, remote signals or barrier semaphores. Data moves between devices by JAX's collectives and lax.ppermute only.
A program may use at most 64 MiB of HBM per device.

v0:
```python
import jax
import jax.numpy as jnp
from jax import lax
from jax.sharding import PartitionSpec as P

K_CHILD = 16
CHILDREN = 8
ROOT_ITERS = 2
CHILD_ITERS = 3


HIGH = lax.Precision.HIGHEST


def times_transpose(left_bf, matrix):
    return lax.dot_general(
        left_bf, matrix, (((1,), (1,)), ((), ())), preferred_element_type=jnp.float32
    )


def body(matrix, labels, root_rows, root_cols, child_rows, child_cols):
    root_w = root_rows
    root_h = root_cols
    for iteration in range(ROOT_ITERS):
        numer_h = jnp.dot(root_w.astype(jnp.bfloat16), matrix, preferred_element_type=jnp.float32)
        gram_w = jnp.dot(root_w, root_w.T, precision=HIGH)
        numer_h, gram_w = lax.psum((numer_h, gram_w), "row")
        root_h = root_h * numer_h / jnp.dot(gram_w, root_h, precision=HIGH)
        numer_w = times_transpose(root_h.astype(jnp.bfloat16), matrix)
        gram_h = jnp.dot(root_h, root_h.T, precision=HIGH)
        numer_w, gram_h = lax.psum((numer_w, gram_h), "col")
        root_w = root_w * numer_w / jnp.dot(gram_h, root_w, precision=HIGH)
    member = (labels[:, 0][None, :] == jnp.arange(CHILDREN, dtype=jnp.int32)[:, None]).astype(
        jnp.float32
    )
    own_weight = jnp.sum(member * root_w, axis=0)
    child_w = child_rows * own_weight[None, :]
    child_h = child_cols * jnp.repeat(root_h, K_CHILD, axis=0)
    total_rows = CHILDREN * K_CHILD
    for iteration in range(CHILD_ITERS):
        spread = member[:, None, :] * child_w[None, :, :]
        spread_bf = spread.reshape(total_rows, -1).astype(jnp.bfloat16)
        numer_ch = jnp.dot(spread_bf, matrix, preferred_element_type=jnp.float32)
        gram_c = jnp.einsum("cjr,ckr->cjk", spread, spread, precision=HIGH)
        numer_ch, gram_c = lax.psum((numer_ch, gram_c), "row")
        blocks = child_h.reshape(CHILDREN, K_CHILD, -1)
        lower = jnp.einsum("cjk,ckn->cjn", gram_c, blocks, precision=HIGH).reshape(total_rows, -1)
        child_h = child_h * numer_ch / lower
        full_rows = times_transpose(child_h.astype(jnp.bfloat16), matrix)
        numer_cw = jnp.sum(full_rows.reshape(CHILDREN, K_CHILD, -1) * member[:, None, :], axis=0)
        blocks = child_h.reshape(CHILDREN, K_CHILD, -1)
        hgram = jnp.einsum("cjn,ckn->cjk", blocks, blocks, precision=HIGH)
        numer_cw, hgram = lax.psum((numer_cw, hgram), "col")
        lower_w = jnp.sum(
            jnp.einsum("cjk,kr->cjr", hgram, child_w, precision=HIGH) * member[:, None, :], axis=0
        )
        child_w = child_w * numer_cw / lower_w
    return (root_w, root_h, child_w, child_h)


def solution(mesh):
    return jax.shard_map(
        body,
        mesh=mesh,
        in_specs=(
            P("row", "col"),
            P("row", None),
            P(None, "row"),
            P(None, "col"),
            P(None, "row"),
            P(None, "col"),
        ),
        out_specs=(P(None, "row"), P(None, "col"), P(None, "row"), P(None, "col")),
        check_vma=False,
    )
```

profile of v0, /device:TPU:0, one launch (start us, length us, event | category | flops | bytes accessed | tf_op | source)
XLA Modules:
  0.0 592.8 jit_solution(2322174769713533654)
XLA Ops:
  7.2 5.3 fusion.31
  12.8 15.2 %psum.141 = f32[8,8]{1,0:T(8,128)S(1)} all-reduce(f32[8,8]{1,0:T(8,128)S(1)} %fusion.33), channel_id=1, replica_groups=mesh['row'=8,'col'=4] {'row'}, use_global_device_ids=true, to_apply=%region_1.0 | all-reduce | flops 64 | bytes 512 | tf_op jit(solution)/shard_map/psum | solution.py:27
  28.0 40.6 %all-reduce.11.cloned.1.call-done = f32[8,2048]{1,0:T(8,128)} async-done(((f32[8,2048]{1,0:T(8,128)}), f32[8,2048]{1,0:T(8,128)}) %all-reduce.11.cloned.1.call-update) | async-done | bytes 65552 | tf_op jit(solution)/shard_map/psum | solution.py:27
  69.6 6.3 %fusion.29 = f32[8,2048]{1,0:T(8,128)} fusion(bf16[2048,2048]{1,0:T(8,128)(2,1)} %param.6, f32[8,2048]{1,0:T(8,128)S(1)} %convolution_divide_fusion.3), kind=kOutput, calls=%fused_computation.52 | convolution fusion | flops 67125248 | bytes 8519680 | tf_op jit(solution)/shard_map/dot_general | solution.py:16
  76.2 11.7 %psum.143 = f32[8,8]{1,0:T(8,128)S(1)} all-reduce(f32[8,8]{1,0:T(8,128)S(1)} %fusion.34), channel_id=1, replica_groups=mesh['row'=8,'col'=4] {'col'}, use_global_device_ids=true, to_apply=%region_3.0 | all-reduce | flops 64 | bytes 512 | tf_op jit(solution)/shard_map/psum | solution.py:31
  87.9 21.9 %all-reduce.13.cloned.1.call-done = f32[8,2048]{1,0:T(8,128)} async-done(((f32[8,2048]{1,0:T(8,128)}), f32[8,2048]{1,0:T(8,128)}) %all-reduce.13.cloned.1.call-update) | async-done | bytes 65552 | tf_op jit(solution)/shard_map/psum | solution.py:31
  110.9 5.2 fusion.27
  116.4 11.8 %psum.145 = f32[8,8]{1,0:T(8,128)S(1)} all-reduce(f32[8,8]{1,0:T(8,128)S(1)} %fusion.35), channel_id=1, replica_groups=mesh['row'=8,'col'=4] {'row'}, use_global_device_ids=true, to_apply=%region_5.0 | all-reduce | flops 64 | bytes 512 | tf_op jit(solution)/shard_map/psum | solution.py:27
  128.2 40.9 %all-reduce.15.cloned.1.call-done = f32[8,2048]{1,0:T(8,128)} async-done(((f32[8,2048]{1,0:T(8,128)}), f32[8,2048]{1,0:T(8,128)}) %all-reduce.15.cloned.1.call-update) | async-done | bytes 65552 | tf_op jit(solution)/shard_map/psum | solution.py:27
  170.2 6.3 %fusion.25 = f32[8,2048]{1,0:T(8,128)} fusion(bf16[2048,2048]{1,0:T(8,128)(2,1)} %param.6, f32[8,2048]{1,0:T(8,128)S(1)} %convolution_divide_fusion.1), kind=kOutput, calls=%fused_computation.48 | convolution fusion | flops 67125248 | bytes 8519680 | tf_op jit(solution)/shard_map/dot_general | solution.py:16
  176.8 11.7 %psum.147 = f32[8,8]{1,0:T(8,128)S(1)} all-reduce(f32[8,8]{1,0:T(8,128)S(1)} %fusion.36), channel_id=1, replica_groups=mesh['row'=8,'col'=4] {'col'}, use_global_device_ids=true, to_apply=%region_7.0 | all-reduce | flops 64 | bytes 512 | tf_op jit(solution)/shard_map/psum | solution.py:31
  188.5 21.9 %all-reduce.17.cloned.1.call-done = f32[8,2048]{1,0:T(8,128)} async-done(((f32[8,2048]{1,0:T(8,128)}), f32[8,2048]{1,0:T(8,128)}) %all-reduce.17.cloned.1.call-update) | async-done | bytes 65552 | tf_op jit(solution)/shard_map/psum | solution.py:31
  210.4 1.7 select_reduce_fusion
  212.2 5.7 fusion.37
  218.1 1.6 fusion.4
  219.8 23.0 %psum.149 = f32[8,16,16]{2,1,0:T(8,128)S(1)} all-reduce(f32[8,16,16]{2,1,0:T(8,128)S(1)} %fusion.4), channel_id=1, replica_groups=mesh['row'=8,'col'=4] {'row'}, use_global_device_ids=true, to_apply=%region_10.0 | all-reduce | flops 2048 | bytes 16384 | tf_op jit(solution)/shard_map/psum | solution.py:45
  243.8 30.8 %all-reduce.19.cloned.1.call-done = f32[128,2048]{1,0:T(8,128)} async-done(((f32[128,2048]{1,0:T(8,128)}), f32[128,2048]{1,0:T(8,128)}) %all-reduce.19.cloned.1.call-update) | async-done | bytes 1048592 | tf_op jit(solution)/shard_map/psum | solution.py:45
  276.1 6.3 %fusion.15 = f32[128,2048]{1,0:T(8,128)S(1)} fusion(bf16[2048,2048]{1,0:T(8,128)(2,1)} %param.6, f32[128,2048]{1,0:T(8,128)S(1)} %bitcast_divide_fusion.2), kind=kOutput, calls=%fused_computation.32 | convolution fusion | flops 1074003968 | bytes 10485760 | tf_op jit(solution)/shard_map/dot_general | solution.py:16
  283.8 19.5 %psum.151 = f32[8,16,16]{2,1,0:T(8,128)S(1)} all-reduce(f32[8,16,16]{2,1,0:T(8,128)S(1)} %fusion.39), channel_id=1, replica_groups=mesh['row'=8,'col'=4] {'col'}, use_global_device_ids=true, to_apply=%region_13.0 | all-reduce | flops 2048 | bytes 16384 | tf_op jit(solution)/shard_map/psum | solution.py:53
  305.1 30.4 %all-reduce.21.cloned.1.call-done = f32[16,2048]{1,0:T(8,128)} async-done(((f32[16,2048]{1,0:T(8,128)}), f32[16,2048]{1,0:T(8,128)}) %all-reduce.21.cloned.1.call-update) | async-done | bytes 131088 | tf_op jit(solution)/shard_map/psum | solution.py:53
  336.5 5.6 fusion.40
  343.9 23.1 %psum.153 = f32[8,16,16]{2,1,0:T(8,128)S(1)} all-reduce(f32[8,16,16]{2,1,0:T(8,128)S(1)} %fusion.2), channel_id=1, replica_groups=mesh['row'=8,'col'=4] {'row'}, use_global_device_ids=true, to_apply=%region_16.0 | all-reduce | flops 2048 | bytes 16384 | tf_op jit(solution)/shard_map/psum | solution.py:45
  368.1 30.8 %all-reduce.23.cloned.1.call-done = f32[128,2048]{1,0:T(8,128)} async-done(((f32[128,2048]{1,0:T(8,128)}), f32[128,2048]{1,0:T(8,128)}) %all-reduce.23.cloned.1.call-update) | async-done | bytes 1048592 | tf_op jit(solution)/shard_map/psum | solution.py:45
  400.4 6.3 %fusion.12 = f32[128,2048]{1,0:T(8,128)S(1)} fusion(bf16[2048,2048]{1,0:T(8,128)(2,1)} %param.6, f32[128,2048]{1,0:T(8,128)S(1)} %bitcast_divide_fusion.1), kind=kOutput, calls=%fused_computation.29 | convolution fusion | flops 1074003968 | bytes 10485760 | tf_op jit(solution)/shard_map/dot_general | solution.py:16
  408.0 19.5 %psum.155 = f32[8,16,16]{2,1,0:T(8,128)S(1)} all-reduce(f32[8,16,16]{2,1,0:T(8,128)S(1)} %fusion.42), channel_id=1, replica_groups=mesh['row'=8,'col'=4] {'col'}, use_global_device_ids=true, to_apply=%region_19.0 | all-reduce | flops 2048 | bytes 16384 | tf_op jit(solution)/shard_map/psum | solution.py:53
  429.4 30.4 %all-reduce.25.cloned.1.call-done = f32[16,2048]{1,0:T(8,128)} async-done(((f32[16,2048]{1,0:T(8,128)}), f32[16,2048]{1,0:T(8,128)}) %all-reduce.25.cloned.1.call-update) | async-done | bytes 131088 | tf_op jit(solution)/shard_map/psum | solution.py:53
  460.8 5.6 fusion.43
  468.1 23.1 %psum.157 = f32[8,16,16]{2,1,0:T(8,128)S(1)} all-reduce(f32[8,16,16]{2,1,0:T(8,128)S(1)} %fusion), channel_id=1, replica_groups=mesh['row'=8,'col'=4] {'row'}, use_global_device_ids=true, to_apply=%region_22.0 | all-reduce | flops 2048 | bytes 16384 | tf_op jit(solution)/shard_map/psum | solution.py:45
  492.3 30.8 %all-reduce.27.cloned.1.call-done = f32[128,2048]{1,0:T(8,128)} async-done(((f32[128,2048]{1,0:T(8,128)}), f32[128,2048]{1,0:T(8,128)}) %all-reduce.27.cloned.1.call-update) | async-done | bytes 1048592 | tf_op jit(solution)/shard_map/psum | solution.py:45
  524.6 6.6 %fusion.9 = f32[128,2048]{1,0:T(8,128)S(1)} fusion(bf16[2048,2048]{1,0:T(8,128)(2,1)} %param.6, f32[128,2048]{1,0:T(8,128)S(1)} %bitcast_divide_fusion), kind=kOutput, calls=%fused_computation.26 | convolution fusion | flops 1074003968 | bytes 10485760 | tf_op jit(solution)/shard_map/dot_general | solution.py:16
  532.7 19.5 %psum.159 = f32[8,16,16]{2,1,0:T(8,128)S(1)} all-reduce(f32[8,16,16]{2,1,0:T(8,128)S(1)} %fusion.45), channel_id=1, replica_groups=mesh['row'=8,'col'=4] {'col'}, use_global_device_ids=true, to_apply=%region_25.0 | all-reduce | flops 2048 | bytes 16384 | tf_op jit(solution)/shard_map/psum | solution.py:53
  554.0 30.5 %all-reduce.29.cloned.1.call-done = f32[16,2048]{1,0:T(8,128)} async-done(((f32[16,2048]{1,0:T(8,128)}), f32[16,2048]{1,0:T(8,128)}) %all-reduce.29.cloned.1.call-update) | async-done | bytes 131088 | tf_op jit(solution)/shard_map/psum | solution.py:53
  (67 shorter events, 28.3 us)
Async XLA Ops:
  7.2 5.5 copy-start.3
  7.2 5.4 copy-start.5
  7.2 61.4 %copy-start.6 = (f32[8,2048]{1,0:T(8,128)S(1)}, f32[8,2048]{1,0:T(8,128)}, u32[]{:S(2)}) copy-start(f32[8,2048]{1,0:T(8,128)} %param.9) | copy-start | bytes 196612
  7.2 61.4 %all-reduce.11.cloned.1.call-start = ((), (), s32[]{:S(2)}) async-start(), calls=%async_computation | async-start | bytes 131072 | tf_op jit(solution)/shard_map/psum | solution.py:27
  12.5 97.3 %all-reduce.13.cloned.1.call-start = ((), (), s32[]{:S(2)}) async-start(), calls=%async_computation.1 | async-start | bytes 131072 | tf_op jit(solution)/shard_map/psum | solution.py:31
  75.9 93.2 %all-reduce.15.cloned.1.call-start = ((), (), s32[]{:S(2)}) async-start(), calls=%async_computation.2 | async-start | bytes 131072 | tf_op jit(solution)/shard_map/psum | solution.py:27
  116.1 96.0 %copy-start.4 = (f32[16,2048]{1,0:T(8,128)S(1)}, f32[16,2048]{1,0:T(8,128)}, u32[]{:S(2)}) copy-start(f32[16,2048]{1,0:T(8,128)} %param.10) | copy-start | bytes 393220
  116.1 94.3 %all-reduce.17.cloned.1.call-start = ((), (), s32[]{:S(2)}) async-start(), calls=%async_computation.3 | async-start | bytes 131072 | tf_op jit(solution)/shard_map/psum | solution.py:31
  170.2 47.8 %copy-start.1 = (f32[8,2048]{1,0:T(8,128)}, f32[8,2048]{1,0:T(8,128)S(1)}, u32[]{:S(2)}) copy-start(f32[8,2048]{1,0:T(8,128)S(1)} %convolution_divide_fusion.1) | copy-start | bytes 196612
  176.5 98.1 %all-reduce.19.cloned.1.call-start = ((), (), s32[]{:S(2)}) async-start(), calls=%async_computation.4 | async-start | bytes 2097152 | tf_op jit(solution)/shard_map/psum | solution.py:45
  212.2 5.8 copy-start.2
  218.0 117.6 %all-reduce.21.cloned.1.call-start = ((), (), s32[]{:S(2)}) async-start(), calls=%async_computation.5 | async-start | bytes 262144 | tf_op jit(solution)/shard_map/psum | solution.py:53
  304.1 94.8 %all-reduce.23.cloned.1.call-start = ((), (), s32[]{:S(2)}) async-start(), calls=%async_computation.6 | async-start | bytes 2097152 | tf_op jit(solution)/shard_map/psum | solution.py:45
  342.2 117.6 %all-reduce.25.cloned.1.call-start = ((), (), s32[]{:S(2)}) async-start(), calls=%async_computation.7 | async-start | bytes 262144 | tf_op jit(solution)/shard_map/psum | solution.py:53
  428.3 94.8 %all-reduce.27.cloned.1.call-start = ((), (), s32[]{:S(2)}) async-start(), calls=%async_computation.8 | async-start | bytes 2097152 | tf_op jit(solution)/shard_map/psum | solution.py:45
  466.5 118.0 %all-reduce.29.cloned.1.call-start = ((), (), s32[]{:S(2)}) async-start(), calls=%async_computation.9 | async-start | bytes 262144 | tf_op jit(solution)/shard_map/psum | solution.py:53
  524.6 61.4 %copy-start = (f32[128,2048]{1,0:T(8,128)}, f32[128,2048]{1,0:T(8,128)S(1)}, u32[]{:S(2)}) copy-start(f32[128,2048]{1,0:T(8,128)S(1)} %bitcast_divide_fusion) | copy-start | bytes 3145732
Sparse Core Ops, SparseCore 0:
  12.7 55.8 all-reduce.10
  76.1 33.7 all-reduce.12
  116.2 52.8 all-reduce.14
  176.7 33.7 all-reduce.16
  218.1 56.5 all-reduce.18
  304.2 31.2 all-reduce.20
  342.3 56.5 all-reduce.22
  428.5 31.2 all-reduce.24
  466.6 56.5 all-reduce.26
  553.1 31.2 all-reduce.28
where the time goes:
time: 594 us; the launch traced here: 593 us
  waiting for transfers between devices  309 us (52%)
  blocking collectives  178 us (30%)
  matrix products  79.8 us (13%)
  between operations  14.5 us (2%)
  other arithmetic  10.4 us (2%)
    psum x3, waiting for transfers between devices, body(): numer_ch, gram_c = lax.psum((numer_ch, gram_c), 'row')  92.5 us
    psum x3, waiting for transfers between devices, body(): numer_cw, hgram = lax.psum((numer_cw, hgram), 'col')  91.3 us
    psum x2, waiting for transfers between devices, body(): numer_h, gram_w = lax.psum((numer_h, gram_w), 'row')  81.5 us
    psum x3, blocking collectives, body(): numer_ch, gram_c = lax.psum((numer_ch, gram_c), 'row')  69.3 us
    psum x3, blocking collectives, body(): numer_cw, hgram = lax.psum((numer_cw, hgram), 'col')  58.6 us
    psum x2, waiting for transfers between devices, body(): numer_w, gram_h = lax.psum((numer_w, gram_h), 'col')  43.8 us
    dot_general x5, matrix products, times_transpose(): lax.dot_general(left_bf, matrix, (((1,), (1,)), ((), ())), preferred_elem...  31.7 us
    psum x2, blocking collectives, body(): numer_h, gram_w = lax.psum((numer_h, gram_w), 'row')  27 us
  transfers between devices with their start and end apart: 10, of which 10 were waited for; matrix products, arithmetic and copies ran while one was open for 2% of the time, Pallas kernels for 0%

commit v1 on v0

v1 whole, which is shorter than its diff:
```python
import jax
import jax.numpy as jnp
from jax import lax
from jax.sharding import PartitionSpec as P

K_CHILD = 16
CHILDREN = 8
ROOT_ITERS = 2
CHILD_ITERS = 3


HIGH = lax.Precision.HIGHEST


def times_transpose(left_bf, matrix):
    return lax.dot_general(
        left_bf, matrix, (((1,), (1,)), ((), ())), preferred_element_type=jnp.float32
    )


def swap(x, axis, size, mask):
    return lax.ppermute(x, axis, [(i, i ^ mask) for i in range(size)])


def masks_of(size):
    return [1 << b for b in range(size.bit_length() - 1)]


def butterfly(x, axis, size, masks):
    masks = list(masks)
    while masks:
        if len(masks) == 1:
            x = x + swap(x, axis, size, masks.pop(0))
            continue
        a, b = masks.pop(0), masks.pop(0)
        xa, xb, xab = (swap(x, axis, size, m) for m in (a, b, a ^ b))
        x = (x + xa) + (xb + xab)
    return x


def sum_rows(x, rows):
    masks = masks_of(rows)
    x = x + swap(x, "row", rows, 1)
    return butterfly(x, "row", rows, masks[1:])


def sum_cols(x, cols):
    return butterfly(x, "col", cols, masks_of(cols))


def make_body(rows, cols):
    def body(matrix, labels, root_rows, root_cols, child_rows, child_cols):
        root_w = root_rows
        root_h = root_cols
        for iteration in range(ROOT_ITERS):
            gram_w = sum_rows(jnp.dot(root_w, root_w.T, precision=HIGH), rows)
            numer_h = jnp.dot(root_w.astype(jnp.bfloat16), matrix, preferred_element_type=jnp.float32)
            numer_h = sum_rows(numer_h, rows)
            root_h = root_h * numer_h / jnp.dot(gram_w, root_h, precision=HIGH)
            gram_h = sum_cols(jnp.dot(root_h, root_h.T, precision=HIGH), cols)
            numer_w = times_transpose(root_h.astype(jnp.bfloat16), matrix)
            numer_w = sum_cols(numer_w, cols)
            root_w = root_w * numer_w / jnp.dot(gram_h, root_w, precision=HIGH)
        member = (labels[:, 0][None, :] == jnp.arange(CHILDREN, dtype=jnp.int32)[:, None]).astype(
            jnp.float32
        )
        own_weight = jnp.sum(member * root_w, axis=0)
        child_w = child_rows * own_weight[None, :]
        total_rows = CHILDREN * K_CHILD
        half = total_rows // 2
        core = lax.axis_index("row") & 1
        child_h = child_cols * jnp.repeat(root_h, K_CHILD, axis=0)
        mine = lax.dynamic_slice_in_dim(child_h, core * half, half, 0)
        masks = masks_of(rows)[1:]
        for iteration in range(CHILD_ITERS):
            spread = member[:, None, :] * child_w[None, :, :]
            spread_bf = spread.reshape(total_rows, -1).astype(jnp.bfloat16)
            gram_c = sum_rows(jnp.einsum("cjr,ckr->cjk", spread, spread, precision=HIGH), rows)
            gram_mine = lax.dynamic_slice_in_dim(gram_c, core * (CHILDREN // 2), CHILDREN // 2, 0)
            blocks = mine.reshape(CHILDREN // 2, K_CHILD, -1)
            lower = jnp.einsum("cjk,ckn->cjn", gram_mine, blocks, precision=HIGH).reshape(half, -1)
            numer_ch = jnp.dot(spread_bf, matrix, preferred_element_type=jnp.float32)
            keep = lax.dynamic_slice_in_dim(numer_ch, core * half, half, 0)
            send = lax.dynamic_slice_in_dim(numer_ch, (1 - core) * half, half, 0)
            part = keep + swap(send, "row", rows, 1)
            first, second = part[: half // 2], part[half // 2 :]
            for a, b in zip(masks, masks[::-1]):
                first, second = (
                    first + swap(first, "row", rows, a),
                    second + swap(second, "row", rows, b),
                )
            mine = mine * jnp.concatenate([first, second]) / lower
            other = swap(mine, "row", rows, 1)
            low, high = jnp.where(core == 0, mine, other), jnp.where(core == 0, other, mine)
            child_h = jnp.concatenate([low, high])
            blocks = child_h.reshape(CHILDREN, K_CHILD, -1)
            hgram = sum_cols(jnp.einsum("cjn,ckn->cjk", blocks, blocks, precision=HIGH), cols)
            full_rows = times_transpose(child_h.astype(jnp.bfloat16), matrix)
            numer_cw = jnp.sum(full_rows.reshape(CHILDREN, K_CHILD, -1) * member[:, None, :], axis=0)
            numer_cw = sum_cols(numer_cw, cols)
            lower_w = jnp.sum(
                jnp.einsum("cjk,kr->cjr", hgram, child_w, precision=HIGH) * member[:, None, :], axis=0
            )
            child_w = child_w * numer_cw / lower_w
        return (root_w, root_h, child_w, child_h)

    return body


def solution(mesh):
    return jax.shard_map(
        make_body(mesh.shape["row"], mesh.shape["col"]),
        mesh=mesh,
        in_specs=(
            P("row", "col"),
            P("row", None),
            P(None, "row"),
            P(None, "col"),
            P(None, "row"),
            P(None, "col"),
        ),
        out_specs=(P(None, "row"), P(None, "col"), P(None, "row"), P(None, "col")),
        check_vma=False,
    )
```

time: 594 us -> 219 us (0.37)
  waiting for transfers between devices: 309 us -> 71.1 us
  blocking collectives: 178 us -> 0 us
  starting transfers between devices: 0.41 us -> 93.7 us
  matrix products: 79.8 us -> 49.5 us
  between operations: 14.5 us -> 1.37 us
  other arithmetic: 10.4 us -> 2.97 us
    psum x10 -> x0, waiting for transfers between devices: 309 us -> none  [the longest x3 92.5 us: body(): numer_ch, gram_c = lax.psum((numer_ch, gram_c), 'row')]
    psum x10 -> x0, blocking collectives: 178 us -> none  [the longest x3 69.3 us: body(): numer_ch, gram_c = lax.psum((numer_ch, gram_c), 'row')]
    ppermute x0 -> x76, starting transfers between devices: none -> 93.7 us  [swap(): return lax.ppermute(x, axis, [(i, i ^ mask) for i in range(size)])]
    ppermute x0 -> x76, waiting for transfers between devices: none -> 71.1 us  [swap(): return lax.ppermute(x, axis, [(i, i ^ mask) for i in range(size)])]
    dot_general x5, matrix products: 31.7 us -> 20.2 us  [times_transpose(): lax.dot_general(left_bf, matrix, (((1,), (1,)), ((), ())), preferred_elem...]
    dot_general x3, matrix products: 17 us -> 7.37 us  [body(): numer_ch = jnp.dot(spread_bf, matrix, preferred_element_type=jnp.float32)]
  transfers between devices with their start and end apart: 10 -> 76, of which waited for: 10 -> 36; matrix products, arithmetic and copies ran while one was open for 2% -> 11% of each run, Pallas kernels for 0% -> 0%
where the time goes in v1:
time: 219 us
  starting transfers between devices  93.7 us (43%)
  waiting for transfers between devices  71.1 us (32%)
  matrix products  49.5 us (23%)
  other arithmetic  2.97 us (1%)
    ppermute x76, starting transfers between devices, swap(): return lax.ppermute(x, axis, [(i, i ^ mask) for i in range(size)])  93.7 us
    ppermute x76, waiting for transfers between devices, swap(): return lax.ppermute(x, axis, [(i, i ^ mask) for i in range(size)])  71.1 us
    dot_general x5, matrix products, times_transpose(): lax.dot_general(left_bf, matrix, (((1,), (1,)), ((), ())), preferred_elem...  20.2 us
    dot_general x3, matrix products, body(): numer_ch = jnp.dot(spread_bf, matrix, preferred_element_type=jnp.float32)  7.37 us
    dot_general x2, matrix products, body(): jnp.dot(root_w.astype(jnp.bfloat16), matrix, preferred_element_type=jnp.f...  5.98 us
    dot_general x3, matrix products, body(): jnp.einsum('cjr,ckr->cjk', spread, spread, precision=HIGH)  5 us
  transfers between devices with their start and end apart: 76, of which 36 were waited for; matrix products, arithmetic and copies ran while one was open for 11% of the time, Pallas kernels for 0%

profile of v1, /device:TPU:0, one launch (start us, length us, event | category | flops | bytes accessed | tf_op | source)
XLA Modules:
  0.0 218.9 jit_solution(6822526361338390561)
XLA Ops:
  0.7 4.8 %fusion.58 = f32[8,2048]{1,0:T(8,128)S(1)} fusion(bf16[2048,2048]{1,0:T(8,128)(2,1)} %param.6, f32[8,2048]{1,0:T(8,128)} %param.8), kind=kOutput, calls=%fused_computation.96 | convolution fusion | flops 67125248 | bytes 8519680 | tf_op jit(solution)/shard_map/dot_general | solution.py:57
  6.9 2.9 %collective-permute-start.2 = (f32[8,2048]{1,0:T(8,128)S(1)}, f32[8,2048]{1,0:T(8,128)S(1)}, u32[]{:S(2)}, u32[]{:S(2)}) collective-permute-start(f32[8,2048]{1,0:T(8,128)S(1)} %add.235), channel_id=1, source_target_pairs={{0,16},{4,20},{8,24},{12,28},{16,0},{20,4},{24,8},{28,12},{1,17},{... | collective-permute-start | bytes 196616 | tf_op jit(solution)/shard_map/ppermute | solution.py:22
  12.7 1.9 collective-permute-start.6
  16.3 1.9 collective-permute-start.5
  20.2 2.3 %fusion.56 = f32[8,2048]{1,0:T(8,128)S(1)} fusion(bf16[2048,2048]{1,0:T(8,128)(2,1)S(1)} %copy-done, f32[8,2048]{1,0:T(8,128)S(1)} %multiply_divide_fusion.6), kind=kOutput, calls=%fused_computation.94 | convolution fusion | flops 67125248 | bytes 8519680 | tf_op jit(solution)/shard_map/dot_general | solution.py:16
  22.5 3.0 %collective-permute-start.9 = (f32[8,2048]{1,0:T(8,128)S(1)}, f32[8,2048]{1,0:T(8,128)S(1)}, u32[]{:S(2)}, u32[]{:S(2)}) collective-permute-start(f32[8,2048]{1,0:T(8,128)S(1)} %fusion.56), channel_id=1, source_target_pairs={{0,2},{1,3},{2,0},{3,1},{4,6},{5,7},{6,4},{7,5},{8,10},{9,11},{10,... | collective-permute-start | bytes 196616 | tf_op jit(solution)/shard_map/ppermute | solution.py:22
  27.3 2.9 %collective-permute-start.12 = (f32[8,8]{1,0:T(8,128)S(1)}, f32[8,8]{1,0:T(8,128)S(1)}, u32[]{:S(2)}, u32[]{:S(2)}) collective-permute-start(f32[8,8]{1,0:T(8,128)S(1)} %fusion.91), channel_id=1, source_target_pairs={{0,2},{1,3},{2,0},{3,1},{4,6},{5,7},{6,4},{7,5},{8,10},{9,11},{10,... | collective-permute-start | bytes 776 | tf_op jit(solution)/shard_map/ppermute | solution.py:22
  40.7 2.4 %collective-permute-start.17 = (f32[8,2048]{1,0:T(8,128)S(1)}, f32[8,2048]{1,0:T(8,128)S(1)}, u32[]{:S(2)}, u32[]{:S(2)}) collective-permute-start(f32[8,2048]{1,0:T(8,128)S(1)} %add.249), channel_id=1, source_target_pairs={{0,24},{4,28},{8,16},{12,20},{16,8},{20,12},{24,0},{28,4},{1,25},{... | collective-permute-start | bytes 196616 | tf_op jit(solution)/shard_map/ppermute | solution.py:22
  45.7 2.5 %collective-permute-done.21 = f32[8,8]{1,0:T(8,128)S(1)} collective-permute-done((f32[8,8]{1,0:T(8,128)S(1)}, f32[8,8]{1,0:T(8,128)S(1)}, u32[]{:S(2)}, u32[]{:S(2)}) %collective-permute-start.21) | collective-permute-done | bytes 288 | tf_op jit(solution)/shard_map/ppermute | solution.py:22
  49.0 5.7 %fusion.52 = f32[8,2048]{1,0:T(8,128)S(1)} fusion(bf16[2048,2048]{1,0:T(8,128)(2,1)} %param.6, f32[8,2048]{1,0:T(8,128)S(1)} %multiply_divide_fusion.4), kind=kOutput, calls=%fused_computation.90 | convolution fusion | flops 67125248 | bytes 8519680 | tf_op jit(solution)/shard_map/dot_general | solution.py:16
  54.7 2.7 %collective-permute-start.23 = (f32[8,2048]{1,0:T(8,128)S(1)}, f32[8,2048]{1,0:T(8,128)S(1)}, u32[]{:S(2)}, u32[]{:S(2)}) collective-permute-start(f32[8,2048]{1,0:T(8,128)S(1)} %fusion.52), channel_id=1, source_target_pairs={{0,2},{1,3},{2,0},{3,1},{4,6},{5,7},{6,4},{7,5},{8,10},{9,11},{10,... | collective-permute-start | bytes 196616 | tf_op jit(solution)/shard_map/ppermute | solution.py:22
  58.9 3.1 %collective-permute-start.26 = (f32[8,8]{1,0:T(8,128)S(1)}, f32[8,8]{1,0:T(8,128)S(1)}, u32[]{:S(2)}, u32[]{:S(2)}) collective-permute-start(f32[8,8]{1,0:T(8,128)S(1)} %fusion.93), channel_id=1, source_target_pairs={{0,2},{1,3},{2,0},{3,1},{4,6},{5,7},{6,4},{7,5},{8,10},{9,11},{10,... | collective-permute-start | bytes 776 | tf_op jit(solution)/shard_map/ppermute | solution.py:22
  65.5 1.9 collective-permute-done.27
  68.4 4.8 %fusion.94 = f32[128,2048]{1,0:T(8,128)S(1)} fusion(bf16[128,2048]{1,0:T(8,128)(2,1)S(1)} %bitcast.74, bf16[2048,2048]{1,0:T(8,128)(2,1)} %param.6), kind=kOutput, calls=%fused_computation.133 | convolution fusion | flops 1073741824 | bytes 9961472 | tf_op jit(solution)/shard_map/dot_general | solution.py:82
  86.8 2.5 %collective-permute-start.30 = (f32[32,2048]{1,0:T(8,128)S(1)}, f32[32,2048]{1,0:T(8,128)S(1)}, u32[]{:S(2)}, u32[]{:S(2)}) collective-permute-start(f32[32,2048]{1,0:T(8,128)S(1)} %get-tuple-element.18), channel_id=1, source_target_pairs={{0,16},{4,20},{8,24},{12,28},{16,0},{20,4},{24,8},{28,12},{1,17},{... | collective-permute-start | bytes 786440 | tf_op jit(solution)/shard_map/ppermute | solution.py:22
  90.0 2.7 %collective-permute-done.32 = f32[32,2048]{1,0:T(8,128)S(1)} collective-permute-done((f32[32,2048]{1,0:T(8,128)S(1)}, f32[32,2048]{1,0:T(8,128)S(1)}, u32[]{:S(2)}, u32[]{:S(2)}) %collective-permute-start.32) | collective-permute-done | bytes 262176 | tf_op jit(solution)/shard_map/ppermute | solution.py:22
  97.3 2.7 %collective-permute-start.42 = (f32[8,16,16]{2,1,0:T(8,128)S(1)}, f32[8,16,16]{2,1,0:T(8,128)S(1)}, u32[]{:S(2)}, u32[]{:S(2)}) collective-permute-start(f32[8,16,16]{2,1,0:T(8,128)S(1)} %fusion.95), channel_id=1, source_target_pairs={{0,2},{1,3},{2,0},{3,1},{4,6},{5,7},{6,4},{7,5},{8,10},{9,11},{10,... | collective-permute-start | bytes 24584 | tf_op jit(solution)/shard_map/ppermute | solution.py:22
  101.4 6.3 %fusion.18 = f32[128,2048]{1,0:T(8,128)S(1)} fusion(bf16[2048,2048]{1,0:T(8,128)(2,1)} %param.6, f32[64,2048]{1,0:T(8,128)S(1)} %get-tuple-element.9, f32[64,2048]{1,0:T(8,128)S(1)} %get-tuple-element.8), kind=kOutput, calls=%fused_computation.36 | convolution fusion | flops 1074790400 | bytes 10485760 | tf_op jit(solution)/shard_map/dot_general | solution.py:16
  107.8 3.1 %collective-permute-start.39 = (f32[16,2048]{1,0:T(8,128)S(1)}, f32[16,2048]{1,0:T(8,128)S(1)}, u32[]{:S(2)}, u32[]{:S(2)}) collective-permute-start(f32[16,2048]{1,0:T(8,128)S(1)} %multiply_reduce_fusion.2), channel_id=1, source_target_pairs={{0,2},{1,3},{2,0},{3,1},{4,6},{5,7},{6,4},{7,5},{8,10},{9,11},{10,... | collective-permute-start | bytes 393224 | tf_op jit(solution)/shard_map/ppermute | solution.py:22
  113.2 7.4 %collective-permute-done.39 = f32[16,2048]{1,0:T(8,128)S(1)} collective-permute-done((f32[16,2048]{1,0:T(8,128)S(1)}, f32[16,2048]{1,0:T(8,128)S(1)}, u32[]{:S(2)}, u32[]{:S(2)}) %collective-permute-start.39) | collective-permute-done | bytes 131104 | tf_op jit(solution)/shard_map/ppermute | solution.py:22
  128.3 4.6 %collective-permute-done.45 = f32[32,2048]{1,0:T(8,128)S(1)} collective-permute-done((f32[32,2048]{1,0:T(8,128)S(1)}, f32[32,2048]{1,0:T(8,128)S(1)}, u32[]{:S(2)}, u32[]{:S(2)}) %collective-permute-start.45) | collective-permute-done | bytes 262176 | tf_op jit(solution)/shard_map/ppermute | solution.py:22
  140.4 3.9 %collective-permute-done.52 = f32[8,16,16]{2,1,0:T(8,128)S(1)} collective-permute-done((f32[8,16,16]{2,1,0:T(8,128)S(1)}, f32[8,16,16]{2,1,0:T(8,128)S(1)}, u32[]{:S(2)}, u32[]{:S(2)}) %collective-permute-start.52) | collective-permute-done | bytes 8224 | tf_op jit(solution)/shard_map/ppermute | solution.py:22
  149.4 2.9 %collective-permute-start.58 = (f32[8,16,16]{2,1,0:T(8,128)S(1)}, f32[8,16,16]{2,1,0:T(8,128)S(1)}, u32[]{:S(2)}, u32[]{:S(2)}) collective-permute-start(f32[8,16,16]{2,1,0:T(8,128)S(1)} %fusion.97), channel_id=1, source_target_pairs={{0,2},{1,3},{2,0},{3,1},{4,6},{5,7},{6,4},{7,5},{8,10},{9,11},{10,... | collective-permute-start | bytes 24584 | tf_op jit(solution)/shard_map/ppermute | solution.py:22
  153.8 3.1 %fusion.15 = f32[128,2048]{1,0:T(8,128)S(1)} fusion(bf16[2048,2048]{1,0:T(8,128)(2,1)S(1)} %bitcast.64, f32[64,2048]{1,0:T(8,128)S(1)} %get-tuple-element.7, f32[64,2048]{1,0:T(8,128)S(1)} %get-tuple-element.6), kind=kOutput, calls=%fused_computation.32 | convolution fusion | flops 1074790400 | bytes 10485760 | tf_op jit(solution)/shard_map/dot_general | solution.py:16
  157.0 3.0 %collective-permute-start.55 = (f32[16,2048]{1,0:T(8,128)S(1)}, f32[16,2048]{1,0:T(8,128)S(1)}, u32[]{:S(2)}, u32[]{:S(2)}) collective-permute-start(f32[16,2048]{1,0:T(8,128)S(1)} %multiply_reduce_fusion.1), channel_id=1, source_target_pairs={{0,2},{1,3},{2,0},{3,1},{4,6},{5,7},{6,4},{7,5},{8,10},{9,11},{10,... | collective-permute-start | bytes 393224 | tf_op jit(solution)/shard_map/ppermute | solution.py:22
  162.5 7.4 %collective-permute-done.55 = f32[16,2048]{1,0:T(8,128)S(1)} collective-permute-done((f32[16,2048]{1,0:T(8,128)S(1)}, f32[16,2048]{1,0:T(8,128)S(1)}, u32[]{:S(2)}, u32[]{:S(2)}) %collective-permute-start.55) | collective-permute-done | bytes 131104 | tf_op jit(solution)/shard_map/ppermute | solution.py:22
  177.4 4.6 %collective-permute-done.61 = f32[32,2048]{1,0:T(8,128)S(1)} collective-permute-done((f32[32,2048]{1,0:T(8,128)S(1)}, f32[32,2048]{1,0:T(8,128)S(1)}, u32[]{:S(2)}, u32[]{:S(2)}) %collective-permute-start.61) | collective-permute-done | bytes 262176 | tf_op jit(solution)/shard_map/ppermute | solution.py:22
  188.9 3.9 %collective-permute-done.68 = f32[8,16,16]{2,1,0:T(8,128)S(1)} collective-permute-done((f32[8,16,16]{2,1,0:T(8,128)S(1)}, f32[8,16,16]{2,1,0:T(8,128)S(1)}, u32[]{:S(2)}, u32[]{:S(2)}) %collective-permute-start.68) | collective-permute-done | bytes 8224 | tf_op jit(solution)/shard_map/ppermute | solution.py:22
  197.9 2.9 %collective-permute-start.74 = (f32[8,16,16]{2,1,0:T(8,128)S(1)}, f32[8,16,16]{2,1,0:T(8,128)S(1)}, u32[]{:S(2)}, u32[]{:S(2)}) collective-permute-start(f32[8,16,16]{2,1,0:T(8,128)S(1)} %fusion.99), channel_id=1, source_target_pairs={{0,2},{1,3},{2,0},{3,1},{4,6},{5,7},{6,4},{7,5},{8,10},{9,11},{10,... | collective-permute-start | bytes 24584 | tf_op jit(solution)/shard_map/ppermute | solution.py:22
  202.3 2.9 %fusion.12 = f32[128,2048]{1,0:T(8,128)S(1)} fusion(bf16[2048,2048]{1,0:T(8,128)(2,1)S(1)} %bitcast.64, f32[128,2048]{1,0:T(8,128)S(1)} %pad_maximum_fusion.2), kind=kOutput, calls=%fused_computation.28 | convolution fusion | flops 1074003968 | bytes 10485760 | tf_op jit(solution)/shard_map/dot_general | solution.py:16
  205.3 3.0 %collective-permute-start.71 = (f32[16,2048]{1,0:T(8,128)S(1)}, f32[16,2048]{1,0:T(8,128)S(1)}, u32[]{:S(2)}, u32[]{:S(2)}) collective-permute-start(f32[16,2048]{1,0:T(8,128)S(1)} %multiply_reduce_fusion), channel_id=1, source_target_pairs={{0,2},{1,3},{2,0},{3,1},{4,6},{5,7},{6,4},{7,5},{8,10},{9,11},{10,... | collective-permute-start | bytes 393224 | tf_op jit(solution)/shard_map/ppermute | solution.py:22
  210.8 7.4 %collective-permute-done.71 = f32[16,2048]{1,0:T(8,128)S(1)} collective-permute-done((f32[16,2048]{1,0:T(8,128)S(1)}, f32[16,2048]{1,0:T(8,128)S(1)}, u32[]{:S(2)}, u32[]{:S(2)}) %collective-permute-start.71) | collective-permute-done | bytes 131104 | tf_op jit(solution)/shard_map/ppermute | solution.py:22
  (218 shorter events, 100.6 us)
Async XLA Ops:
  6.9 13.1 %collective-permute-start.2 = (f32[8,2048]{1,0:T(8,128)S(1)}, f32[8,2048]{1,0:T(8,128)S(1)}, u32[]{:S(2)}, u32[]{:S(2)}) collective-permute-start(f32[8,2048]{1,0:T(8,128)S(1)} %add.235), channel_id=1, source_target_pairs={{0,16},{4,20},{8,24},{12,28},{16,0},{20,4},{24,8},{28,12},{1,17},{... | collective-permute-start | bytes 196616 | tf_op jit(solution)/shard_map/ppermute | solution.py:22
  9.8 10.2 %collective-permute-start.3 = (f32[8,2048]{1,0:T(8,128)S(1)}, f32[8,2048]{1,0:T(8,128)S(1)}, u32[]{:S(2)}, u32[]{:S(2)}) collective-permute-start(f32[8,2048]{1,0:T(8,128)S(1)} %add.235), channel_id=1, source_target_pairs={{0,24},{4,28},{8,16},{12,20},{16,8},{20,12},{24,0},{28,4},{1,25},{... | collective-permute-start | bytes 196616 | tf_op jit(solution)/shard_map/ppermute | solution.py:22
  11.2 8.8 %collective-permute-start.1 = (f32[8,2048]{1,0:T(8,128)S(1)}, f32[8,2048]{1,0:T(8,128)S(1)}, u32[]{:S(2)}, u32[]{:S(2)}) collective-permute-start(f32[8,2048]{1,0:T(8,128)S(1)} %add.235), channel_id=1, source_target_pairs={{0,8},{4,12},{8,0},{12,4},{16,24},{20,28},{24,16},{28,20},{1,9},{5... | collective-permute-start | bytes 196616 | tf_op jit(solution)/shard_map/ppermute | solution.py:22
  22.5 13.1 %collective-permute-start.9 = (f32[8,2048]{1,0:T(8,128)S(1)}, f32[8,2048]{1,0:T(8,128)S(1)}, u32[]{:S(2)}, u32[]{:S(2)}) collective-permute-start(f32[8,2048]{1,0:T(8,128)S(1)} %fusion.56), channel_id=1, source_target_pairs={{0,2},{1,3},{2,0},{3,1},{4,6},{5,7},{6,4},{7,5},{8,10},{9,11},{10,... | collective-permute-start | bytes 196616 | tf_op jit(solution)/shard_map/ppermute | solution.py:22
  25.5 10.1 %collective-permute-start.10 = (f32[8,2048]{1,0:T(8,128)S(1)}, f32[8,2048]{1,0:T(8,128)S(1)}, u32[]{:S(2)}, u32[]{:S(2)}) collective-permute-start(f32[8,2048]{1,0:T(8,128)S(1)} %fusion.56), channel_id=1, source_target_pairs={{0,3},{1,2},{2,1},{3,0},{4,7},{5,6},{6,5},{7,4},{8,11},{9,10},{10,... | collective-permute-start | bytes 196616 | tf_op jit(solution)/shard_map/ppermute | solution.py:22
  26.8 8.7 %collective-permute-start.8 = (f32[8,2048]{1,0:T(8,128)S(1)}, f32[8,2048]{1,0:T(8,128)S(1)}, u32[]{:S(2)}, u32[]{:S(2)}) collective-permute-start(f32[8,2048]{1,0:T(8,128)S(1)} %fusion.56), channel_id=1, source_target_pairs={{0,1},{1,0},{2,3},{3,2},{4,5},{5,4},{6,7},{7,6},{8,9},{9,8},{10,11... | collective-permute-start | bytes 196616 | tf_op jit(solution)/shard_map/ppermute | solution.py:22
  40.1 8.7 %collective-permute-start.16 = (f32[8,2048]{1,0:T(8,128)S(1)}, f32[8,2048]{1,0:T(8,128)S(1)}, u32[]{:S(2)}, u32[]{:S(2)}) collective-permute-start(f32[8,2048]{1,0:T(8,128)S(1)} %add.249), channel_id=1, source_target_pairs={{0,16},{4,20},{8,24},{12,28},{16,0},{20,4},{24,8},{28,12},{1,17},{... | collective-permute-start | bytes 196616 | tf_op jit(solution)/shard_map/ppermute | solution.py:22
  54.7 12.8 %collective-permute-start.23 = (f32[8,2048]{1,0:T(8,128)S(1)}, f32[8,2048]{1,0:T(8,128)S(1)}, u32[]{:S(2)}, u32[]{:S(2)}) collective-permute-start(f32[8,2048]{1,0:T(8,128)S(1)} %fusion.52), channel_id=1, source_target_pairs={{0,2},{1,3},{2,0},{3,1},{4,6},{5,7},{6,4},{7,5},{8,10},{9,11},{10,... | collective-permute-start | bytes 196616 | tf_op jit(solution)/shard_map/ppermute | solution.py:22
  57.4 10.1 %collective-permute-start.24 = (f32[8,2048]{1,0:T(8,128)S(1)}, f32[8,2048]{1,0:T(8,128)S(1)}, u32[]{:S(2)}, u32[]{:S(2)}) collective-permute-start(f32[8,2048]{1,0:T(8,128)S(1)} %fusion.52), channel_id=1, source_target_pairs={{0,3},{1,2},{2,1},{3,0},{4,7},{5,6},{6,5},{7,4},{8,11},{9,10},{10,... | collective-permute-start | bytes 196616 | tf_op jit(solution)/shard_map/ppermute | solution.py:22
  58.8 8.7 %collective-permute-start.22 = (f32[8,2048]{1,0:T(8,128)S(1)}, f32[8,2048]{1,0:T(8,128)S(1)}, u32[]{:S(2)}, u32[]{:S(2)}) collective-permute-start(f32[8,2048]{1,0:T(8,128)S(1)} %fusion.52), channel_id=1, source_target_pairs={{0,1},{1,0},{2,3},{3,2},{4,5},{5,4},{6,7},{7,6},{8,9},{9,8},{10,11... | collective-permute-start | bytes 196616 | tf_op jit(solution)/shard_map/ppermute | solution.py:22
  75.3 8.7 %collective-permute-start.29 = (f32[32,2048]{1,0:T(8,128)S(1)}, f32[32,2048]{1,0:T(8,128)S(1)}, u32[]{:S(2)}, u32[]{:S(2)}) collective-permute-start(f32[32,2048]{1,0:T(8,128)S(1)} %get-tuple-element.20), channel_id=1, source_target_pairs={{0,8},{4,12},{8,0},{12,4},{16,24},{20,28},{24,16},{28,20},{1,9},{5... | collective-permute-start | bytes 786440 | tf_op jit(solution)/shard_map/ppermute | solution.py:22
  80.5 9.0 %collective-permute-start.36 = (f32[8,16,16]{2,1,0:T(8,128)S(1)}, f32[8,16,16]{2,1,0:T(8,128)S(1)}, u32[]{:S(2)}, u32[]{:S(2)}) collective-permute-start(f32[8,16,16]{2,1,0:T(8,128)S(1)} %add.270), channel_id=1, source_target_pairs={{0,24},{4,28},{8,16},{12,20},{16,8},{20,12},{24,0},{28,4},{1,25},{... | collective-permute-start | bytes 24584 | tf_op jit(solution)/shard_map/ppermute | solution.py:22
  97.3 14.9 %collective-permute-start.42 = (f32[8,16,16]{2,1,0:T(8,128)S(1)}, f32[8,16,16]{2,1,0:T(8,128)S(1)}, u32[]{:S(2)}, u32[]{:S(2)}) collective-permute-start(f32[8,16,16]{2,1,0:T(8,128)S(1)} %fusion.95), channel_id=1, source_target_pairs={{0,2},{1,3},{2,0},{3,1},{4,6},{5,7},{6,4},{7,5},{8,10},{9,11},{10,... | collective-permute-start | bytes 24584 | tf_op jit(solution)/shard_map/ppermute | solution.py:22
  100.0 12.2 %collective-permute-start.43 = (f32[8,16,16]{2,1,0:T(8,128)S(1)}, f32[8,16,16]{2,1,0:T(8,128)S(1)}, u32[]{:S(2)}, u32[]{:S(2)}) collective-permute-start(f32[8,16,16]{2,1,0:T(8,128)S(1)} %fusion.95), channel_id=1, source_target_pairs={{0,3},{1,2},{2,1},{3,0},{4,7},{5,6},{6,5},{7,4},{8,11},{9,10},{10,... | collective-permute-start | bytes 24584 | tf_op jit(solution)/shard_map/ppermute | solution.py:22
  101.4 10.9 %collective-permute-start.41 = (f32[8,16,16]{2,1,0:T(8,128)S(1)}, f32[8,16,16]{2,1,0:T(8,128)S(1)}, u32[]{:S(2)}, u32[]{:S(2)}) collective-permute-start(f32[8,16,16]{2,1,0:T(8,128)S(1)} %fusion.95), channel_id=1, source_target_pairs={{0,1},{1,0},{2,3},{3,2},{4,5},{5,4},{6,7},{7,6},{8,9},{9,8},{10,11... | collective-permute-start | bytes 24584 | tf_op jit(solution)/shard_map/ppermute | solution.py:22
  107.8 12.8 %collective-permute-start.39 = (f32[16,2048]{1,0:T(8,128)S(1)}, f32[16,2048]{1,0:T(8,128)S(1)}, u32[]{:S(2)}, u32[]{:S(2)}) collective-permute-start(f32[16,2048]{1,0:T(8,128)S(1)} %multiply_reduce_fusion.2), channel_id=1, source_target_pairs={{0,2},{1,3},{2,0},{3,1},{4,6},{5,7},{6,4},{7,5},{8,10},{9,11},{10,... | collective-permute-start | bytes 393224 | tf_op jit(solution)/shard_map/ppermute | solution.py:22
  110.9 9.7 %collective-permute-start.40 = (f32[16,2048]{1,0:T(8,128)S(1)}, f32[16,2048]{1,0:T(8,128)S(1)}, u32[]{:S(2)}, u32[]{:S(2)}) collective-permute-start(f32[16,2048]{1,0:T(8,128)S(1)} %multiply_reduce_fusion.2), channel_id=1, source_target_pairs={{0,3},{1,2},{2,1},{3,0},{4,7},{5,6},{6,5},{7,4},{8,11},{9,10},{10,... | collective-permute-start | bytes 393224 | tf_op jit(solution)/shard_map/ppermute | solution.py:22
  112.2 8.6 %collective-permute-start.38 = (f32[16,2048]{1,0:T(8,128)S(1)}, f32[16,2048]{1,0:T(8,128)S(1)}, u32[]{:S(2)}, u32[]{:S(2)}) collective-permute-start(f32[16,2048]{1,0:T(8,128)S(1)} %multiply_reduce_fusion.2), channel_id=1, source_target_pairs={{0,1},{1,0},{2,3},{3,2},{4,5},{5,4},{6,7},{7,6},{8,9},{9,8},{10,11... | collective-permute-start | bytes 393224 | tf_op jit(solution)/shard_map/ppermute | solution.py:22
  128.3 8.5 %collective-permute-start.49 = (f32[8,16,16]{2,1,0:T(8,128)S(1)}, f32[8,16,16]{2,1,0:T(8,128)S(1)}, u32[]{:S(2)}, u32[]{:S(2)}) collective-permute-start(f32[8,16,16]{2,1,0:T(8,128)S(1)} %fusion.2), channel_id=1, source_target_pairs={{0,4},{4,0},{8,12},{12,8},{16,20},{20,16},{24,28},{28,24},{1,5},{5... | collective-permute-start | bytes 24584 | tf_op jit(solution)/shard_map/ppermute | solution.py:22
  133.3 12.3 %collective-permute-start.48 = (f32[32,2048]{1,0:T(8,128)S(1)}, f32[32,2048]{1,0:T(8,128)S(1)}, u32[]{:S(2)}, u32[]{:S(2)}) collective-permute-start(f32[32,2048]{1,0:T(8,128)S(1)} %get-tuple-element.15), channel_id=1, source_target_pairs={{0,8},{4,12},{8,0},{12,4},{16,24},{20,28},{24,16},{28,20},{1,9},{5... | collective-permute-start | bytes 786440 | tf_op jit(solution)/shard_map/ppermute | solution.py:22
  135.0 10.6 %collective-permute-start.46 = (f32[32,2048]{1,0:T(8,128)S(1)}, f32[32,2048]{1,0:T(8,128)S(1)}, u32[]{:S(2)}, u32[]{:S(2)}) collective-permute-start(f32[32,2048]{1,0:T(8,128)S(1)} %get-tuple-element.14), channel_id=1, source_target_pairs={{0,16},{4,20},{8,24},{12,28},{16,0},{20,4},{24,8},{28,12},{1,17},{... | collective-permute-start | bytes 786440 | tf_op jit(solution)/shard_map/ppermute | solution.py:22
  149.4 12.1 %collective-permute-start.58 = (f32[8,16,16]{2,1,0:T(8,128)S(1)}, f32[8,16,16]{2,1,0:T(8,128)S(1)}, u32[]{:S(2)}, u32[]{:S(2)}) collective-permute-start(f32[8,16,16]{2,1,0:T(8,128)S(1)} %fusion.97), channel_id=1, source_target_pairs={{0,2},{1,3},{2,0},{3,1},{4,6},{5,7},{6,4},{7,5},{8,10},{9,11},{10,... | collective-permute-start | bytes 24584 | tf_op jit(solution)/shard_map/ppermute | solution.py:22
  152.3 9.2 %collective-permute-start.59 = (f32[8,16,16]{2,1,0:T(8,128)S(1)}, f32[8,16,16]{2,1,0:T(8,128)S(1)}, u32[]{:S(2)}, u32[]{:S(2)}) collective-permute-start(f32[8,16,16]{2,1,0:T(8,128)S(1)} %fusion.97), channel_id=1, source_target_pairs={{0,3},{1,2},{2,1},{3,0},{4,7},{5,6},{6,5},{7,4},{8,11},{9,10},{10,... | collective-permute-start | bytes 24584 | tf_op jit(solution)/shard_map/ppermute | solution.py:22
  157.0 12.8 %collective-permute-start.55 = (f32[16,2048]{1,0:T(8,128)S(1)}, f32[16,2048]{1,0:T(8,128)S(1)}, u32[]{:S(2)}, u32[]{:S(2)}) collective-permute-start(f32[16,2048]{1,0:T(8,128)S(1)} %multiply_reduce_fusion.1), channel_id=1, source_target_pairs={{0,2},{1,3},{2,0},{3,1},{4,6},{5,7},{6,4},{7,5},{8,10},{9,11},{10,... | collective-permute-start | bytes 393224 | tf_op jit(solution)/shard_map/ppermute | solution.py:22
  160.0 9.9 %collective-permute-start.56 = (f32[16,2048]{1,0:T(8,128)S(1)}, f32[16,2048]{1,0:T(8,128)S(1)}, u32[]{:S(2)}, u32[]{:S(2)}) collective-permute-start(f32[16,2048]{1,0:T(8,128)S(1)} %multiply_reduce_fusion.1), channel_id=1, source_target_pairs={{0,3},{1,2},{2,1},{3,0},{4,7},{5,6},{6,5},{7,4},{8,11},{9,10},{10,... | collective-permute-start | bytes 393224 | tf_op jit(solution)/shard_map/ppermute | solution.py:22
  161.5 8.5 %collective-permute-start.54 = (f32[16,2048]{1,0:T(8,128)S(1)}, f32[16,2048]{1,0:T(8,128)S(1)}, u32[]{:S(2)}, u32[]{:S(2)}) collective-permute-start(f32[16,2048]{1,0:T(8,128)S(1)} %multiply_reduce_fusion.1), channel_id=1, source_target_pairs={{0,1},{1,0},{2,3},{3,2},{4,5},{5,4},{6,7},{7,6},{8,9},{9,8},{10,11... | collective-permute-start | bytes 393224 | tf_op jit(solution)/shard_map/ppermute | solution.py:22
  182.2 11.9 %collective-permute-start.64 = (f32[32,2048]{1,0:T(8,128)S(1)}, f32[32,2048]{1,0:T(8,128)S(1)}, u32[]{:S(2)}, u32[]{:S(2)}) collective-permute-start(f32[32,2048]{1,0:T(8,128)S(1)} %get-tuple-element.11), channel_id=1, source_target_pairs={{0,8},{4,12},{8,0},{12,4},{16,24},{20,28},{24,16},{28,20},{1,9},{5... | collective-permute-start | bytes 786440 | tf_op jit(solution)/shard_map/ppermute | solution.py:22
  183.8 10.4 %collective-permute-start.62 = (f32[32,2048]{1,0:T(8,128)S(1)}, f32[32,2048]{1,0:T(8,128)S(1)}, u32[]{:S(2)}, u32[]{:S(2)}) collective-permute-start(f32[32,2048]{1,0:T(8,128)S(1)} %get-tuple-element.10), channel_id=1, source_target_pairs={{0,16},{4,20},{8,24},{12,28},{16,0},{20,4},{24,8},{28,12},{1,17},{... | collective-permute-start | bytes 786440 | tf_op jit(solution)/shard_map/ppermute | solution.py:22
  197.9 11.9 %collective-permute-start.74 = (f32[8,16,16]{2,1,0:T(8,128)S(1)}, f32[8,16,16]{2,1,0:T(8,128)S(1)}, u32[]{:S(2)}, u32[]{:S(2)}) collective-permute-start(f32[8,16,16]{2,1,0:T(8,128)S(1)} %fusion.99), channel_id=1, source_target_pairs={{0,2},{1,3},{2,0},{3,1},{4,6},{5,7},{6,4},{7,5},{8,10},{9,11},{10,... | collective-permute-start | bytes 24584 | tf_op jit(solution)/shard_map/ppermute | solution.py:22
  200.8 9.0 %collective-permute-start.75 = (f32[8,16,16]{2,1,0:T(8,128)S(1)}, f32[8,16,16]{2,1,0:T(8,128)S(1)}, u32[]{:S(2)}, u32[]{:S(2)}) collective-permute-start(f32[8,16,16]{2,1,0:T(8,128)S(1)} %fusion.99), channel_id=1, source_target_pairs={{0,3},{1,2},{2,1},{3,0},{4,7},{5,6},{6,5},{7,4},{8,11},{9,10},{10,... | collective-permute-start | bytes 24584 | tf_op jit(solution)/shard_map/ppermute | solution.py:22
  205.3 12.8 %collective-permute-start.71 = (f32[16,2048]{1,0:T(8,128)S(1)}, f32[16,2048]{1,0:T(8,128)S(1)}, u32[]{:S(2)}, u32[]{:S(2)}) collective-permute-start(f32[16,2048]{1,0:T(8,128)S(1)} %multiply_reduce_fusion), channel_id=1, source_target_pairs={{0,2},{1,3},{2,0},{3,1},{4,6},{5,7},{6,4},{7,5},{8,10},{9,11},{10,... | collective-permute-start | bytes 393224 | tf_op jit(solution)/shard_map/ppermute | solution.py:22
  208.3 9.9 %collective-permute-start.72 = (f32[16,2048]{1,0:T(8,128)S(1)}, f32[16,2048]{1,0:T(8,128)S(1)}, u32[]{:S(2)}, u32[]{:S(2)}) collective-permute-start(f32[16,2048]{1,0:T(8,128)S(1)} %multiply_reduce_fusion), channel_id=1, source_target_pairs={{0,3},{1,2},{2,1},{3,0},{4,7},{5,6},{6,5},{7,4},{8,11},{9,10},{10,... | collective-permute-start | bytes 393224 | tf_op jit(solution)/shard_map/ppermute | solution.py:22
  (54 other events, 467.2 us)

commit v2 on v1

v2 whole, which is shorter than its diff:
```python
import jax
import jax.numpy as jnp
from jax import lax
from jax.sharding import PartitionSpec as P

K_CHILD = 16
CHILDREN = 8
ROOT_ITERS = 2
CHILD_ITERS = 3
LANES = 128
TOTAL = CHILDREN * K_CHILD

HIGH = lax.Precision.HIGHEST


def times_transpose(left_bf, matrix):
    return lax.dot_general(
        left_bf, matrix, (((1,), (1,)), ((), ())), preferred_element_type=jnp.float32
    )


def outer(a, b):
    return lax.dot_general(
        a, b, (((1,), (1,)), ((), ())), precision=HIGH, preferred_element_type=jnp.float32
    )


def swap(x, axis, size, mask):
    return lax.ppermute(x, axis, [(i, i ^ mask) for i in range(size)])


def masks_of(size):
    return [1 << b for b in range(size.bit_length() - 1)]


def butterfly(x, axis, size, masks):
    masks = list(masks)
    while masks:
        if len(masks) == 1:
            x = x + swap(x, axis, size, masks.pop(0))
            continue
        a, b = masks.pop(0), masks.pop(0)
        xa, xb, xab = (swap(x, axis, size, m) for m in (a, b, a ^ b))
        x = (x + xa) + (xb + xab)
    return x


def crossing(first, second, axis, size, masks):
    for a, b in zip(masks, masks[::-1]):
        first, second = (
            first + swap(first, axis, size, a),
            second + swap(second, axis, size, b),
        )
    return first, second


def pad_lanes(x):
    return jnp.pad(x, ((0, 0), (0, LANES - x.shape[1])))


def make_body(rows, cols):
    row_masks, col_masks = masks_of(rows), masks_of(cols)

    def sum_rows(x):
        x = x + swap(x, "row", rows, 1)
        return butterfly(x, "row", rows, row_masks[1:])

    def sum_cols(x):
        return butterfly(x, "col", cols, col_masks)

    def body(matrix, labels, root_rows, root_cols, child_rows, child_cols):
        odd = jnp.broadcast_to(lax.axis_index("row") & 1, (8, LANES))
        odd, root_rows = lax.optimization_barrier((odd, root_rows))
        is_odd = odd[:1, :1] == 1
        nodes, bins = matrix.shape
        k_root = root_rows.shape[0]

        def round_root(own, numer, reduce, width):
            packed = jnp.concatenate([numer, pad_lanes(outer(own, own))], axis=1)
            packed = reduce(packed)
            return packed[:, :width], packed[:, width : width + k_root]

        root_w, root_h = root_rows, root_cols
        for iteration in range(ROOT_ITERS):
            numer = jnp.dot(root_w.astype(jnp.bfloat16), matrix, preferred_element_type=jnp.float32)
            numer, gram = round_root(root_w, numer, sum_rows, bins)
            root_h = root_h * numer / jnp.dot(gram, root_h, precision=HIGH)
            numer = times_transpose(root_h.astype(jnp.bfloat16), matrix)
            numer, gram = round_root(root_h, numer, sum_cols, nodes)
            root_w = root_w * numer / jnp.dot(gram, root_w, precision=HIGH)

        member = (labels[:, 0][None, :] == jnp.arange(CHILDREN, dtype=jnp.int32)[:, None]).astype(
            jnp.float32
        )
        child_w = child_rows * jnp.sum(member * root_w, axis=0)[None, :]
        child_h = child_cols * jnp.repeat(root_h, K_CHILD, axis=0)
        quarter = TOTAL // 4
        pieces = [child_h[i * quarter : (i + 1) * quarter] for i in range(4)]
        mine = [jnp.where(is_odd, pieces[i + 2], pieces[i]) for i in range(2)]
        same = (
            jnp.arange(TOTAL, dtype=jnp.int32)[None, :] // K_CHILD
            == jnp.arange(CHILDREN, dtype=jnp.int32)[:, None]
        ).astype(jnp.float32)
        for iteration in range(CHILD_ITERS):
            spread = (member[:, None, :] * child_w[None, :, :]).reshape(TOTAL, nodes)
            gram = outer(spread, child_w)
            numer = jnp.dot(spread.astype(jnp.bfloat16), matrix, preferred_element_type=jnp.float32)
            packed = jnp.concatenate([numer, pad_lanes(gram)], axis=1)
            pieces = [packed[i * quarter : (i + 1) * quarter] for i in range(4)]
            parts = []
            for i in range(2):
                keep = jnp.where(is_odd, pieces[i + 2], pieces[i])
                send = jnp.where(is_odd, pieces[i], pieces[i + 2])
                parts.append(keep + swap(send, "row", rows, 1))
            parts = crossing(*parts, "row", rows, row_masks[1:])
            low, high = [], []
            for i in range(2):
                gram = parts[i][:, bins : bins + K_CHILD].reshape(-1, K_CHILD, K_CHILD)
                blocks = mine[i].reshape(-1, K_CHILD, bins)
                lower = jnp.einsum("cjk,ckn->cjn", gram, blocks, precision=HIGH).reshape(quarter, bins)
                mine[i] = mine[i] * parts[i][:, :bins] / lower
                other = swap(mine[i], "row", rows, 1)
                low.append(jnp.where(is_odd, other, mine[i]))
                high.append(jnp.where(is_odd, mine[i], other))
            child_h = jnp.concatenate(low + high)
            full = outer(child_h, child_h).reshape(CHILDREN, K_CHILD, TOTAL)
            gram = jnp.sum(full * same[:, None, :], axis=0)
            numer = times_transpose(child_h.astype(jnp.bfloat16), matrix)
            numer = jnp.sum(numer.reshape(CHILDREN, K_CHILD, nodes) * member[:, None, :], axis=0)
            packed = jnp.concatenate([numer, gram], axis=1)
            half = K_CHILD // 2
            packed = jnp.concatenate(crossing(packed[:half], packed[half:], "col", cols, col_masks))
            lower = jnp.dot(packed[:, nodes:], spread, precision=HIGH)
            child_w = child_w * packed[:, :nodes] / lower
        return (root_w, root_h, child_w, child_h)

    return body


def solution(mesh):
    return jax.shard_map(
        make_body(mesh.shape["row"], mesh.shape["col"]),
        mesh=mesh,
        in_specs=(
            P("row", "col"),
            P("row", None),
            P(None, "row"),
            P(None, "col"),
            P(None, "row"),
            P(None, "col"),
        ),
        out_specs=(P(None, "row"), P(None, "col"), P(None, "row"), P(None, "col")),
        check_vma=False,
    )
```

time: 219 us -> 181 us (0.83)
  starting transfers between devices: 93.7 us -> 46.5 us
  waiting for transfers between devices: 71.1 us -> 92.3 us
  matrix products: 49.5 us -> 37.1 us
    ppermute x76 -> x50, starting transfers between devices: 93.7 us -> 46.5 us  [swap(): return lax.ppermute(x, axis, [(i, i ^ mask) for i in range(size)])]
    ppermute x76 -> x50, waiting for transfers between devices: 71.1 us -> 92.3 us  [swap(): return lax.ppermute(x, axis, [(i, i ^ mask) for i in range(size)])]
    dot_general x5, matrix products: 20.2 us -> 13.2 us  [times_transpose(): lax.dot_general(left_bf, matrix, (((1,), (1,)), ((), ())), preferred_elem...]
    dot_general x23 -> x26, matrix products: 23.3 us -> 17.7 us  [the longest x10 7.5 us: outer(): lax.dot_general(a, b, (((1,), (1,)), ((), ())), precision=HIGH, preferred...]
  transfers between devices with their start and end apart: 76 -> 50, of which waited for: 36 -> 45; matrix products, arithmetic and copies ran while one was open for 11% -> 2% of each run, Pallas kernels for 0% -> 0%
where the time goes in v2:
time: 181 us
  waiting for transfers between devices  92.3 us (51%)
  starting transfers between devices  46.5 us (26%)
  matrix products  37.1 us (20%)
  other arithmetic  2.7 us (1%)
  between operations  2.04 us (1%)
    ppermute x50, waiting for transfers between devices, swap(): return lax.ppermute(x, axis, [(i, i ^ mask) for i in range(size)])  92.3 us
    ppermute x50, starting transfers between devices, swap(): return lax.ppermute(x, axis, [(i, i ^ mask) for i in range(size)])  46.5 us
    dot_general x5, matrix products, times_transpose(): lax.dot_general(left_bf, matrix, (((1,), (1,)), ((), ())), preferred_elem...  13.2 us
    dot_general x10, matrix products, outer(): lax.dot_general(a, b, (((1,), (1,)), ((), ())), precision=HIGH, preferred...  7.5 us
    dot_general x2, matrix products, body(): jnp.dot(root_w.astype(jnp.bfloat16), matrix, preferred_element_type=jnp.f...  6.07 us
    dot_general x3, matrix products, body(): jnp.dot(spread.astype(jnp.bfloat16), matrix, preferred_element_type=jnp.f...  3.79 us
  transfers between devices with their start and end apart: 50, of which 45 were waited for; matrix products, arithmetic and copies ran while one was open for 2% of the time, Pallas kernels for 0%

profile of v2, /device:TPU:0, one launch (start us, length us, event | category | flops | bytes accessed | tf_op | source)
XLA Modules:
  0.0 181.2 jit_solution(14596420968022404927)
XLA Ops:
  1.8 4.8 %fusion.45 = f32[8,2048]{1,0:T(8,128)S(1)} fusion(bf16[2048,2048]{1,0:T(8,128)(2,1)} %param.6, f32[8,2048]{1,0:T(8,128)} %param.8), kind=kOutput, calls=%fused_computation.123 | convolution fusion | flops 67125248 | bytes 8519680 | tf_op jit(solution)/shard_map/dot_general | solution.py:85
  8.1 3.8 %collective-permute-start.3 = (f32[8,2176]{1,0:T(8,128)S(1)}, f32[8,2176]{1,0:T(8,128)S(1)}, u32[]{:S(2)}, u32[]{:S(2)}) collective-permute-start(f32[8,2176]{1,0:T(8,128)S(1)} %fusion.77), channel_id=1, source_target_pairs={{0,24},{4,28},{8,16},{12,20},{16,8},{20,12},{24,0},{28,4},{1,25},{... | collective-permute-start | bytes 208904 | tf_op jit(solution)/shard_map/ppermute | solution.py:29
  12.6 1.9 %collective-permute-done.3 = f32[8,2176]{1,0:T(8,128)S(1)} collective-permute-done((f32[8,2176]{1,0:T(8,128)S(1)}, f32[8,2176]{1,0:T(8,128)S(1)}, u32[]{:S(2)}, u32[]{:S(2)}) %collective-permute-start.3) | collective-permute-done | bytes 69664 | tf_op jit(solution)/shard_map/ppermute | solution.py:29
  14.4 1.8 collective-permute-done.2
  17.2 2.3 %fusion.43 = f32[8,2048]{1,0:T(8,128)S(1)} fusion(bf16[2048,2048]{1,0:T(8,128)(2,1)S(1)} %copy-done, f32[8,2048]{1,0:T(8,128)S(1)} %fusion.37), kind=kOutput, calls=%fused_computation.121 | convolution fusion | flops 67125248 | bytes 8519680 | tf_op jit(solution)/shard_map/dot_general | solution.py:17
  19.5 2.7 %collective-permute-start.5 = (f32[8,2176]{1,0:T(8,128)S(1)}, f32[8,2176]{1,0:T(8,128)S(1)}, u32[]{:S(2)}, u32[]{:S(2)}) collective-permute-start(f32[8,2176]{1,0:T(8,128)S(1)} %select_maximum_fusion.5), channel_id=1, source_target_pairs={{0,2},{1,3},{2,0},{3,1},{4,6},{5,7},{6,4},{7,5},{8,10},{9,11},{10,... | collective-permute-start | bytes 208904 | tf_op jit(solution)/shard_map/ppermute | solution.py:29
  23.8 3.0 %collective-permute-done.5 = f32[8,2176]{1,0:T(8,128)S(1)} collective-permute-done((f32[8,2176]{1,0:T(8,128)S(1)}, f32[8,2176]{1,0:T(8,128)S(1)}, u32[]{:S(2)}, u32[]{:S(2)}) %collective-permute-start.5) | collective-permute-done | bytes 69664 | tf_op jit(solution)/shard_map/ppermute | solution.py:29
  26.7 1.7 collective-permute-done.6
  35.2 1.8 collective-permute-done.10
  39.2 2.3 %fusion.39 = f32[8,2048]{1,0:T(8,128)S(1)} fusion(bf16[2048,2048]{1,0:T(8,128)(2,1)S(1)} %copy-done, f32[8,2048]{1,0:T(8,128)S(1)} %fusion.35), kind=kOutput, calls=%fused_computation.117 | convolution fusion | flops 67125248 | bytes 8519680 | tf_op jit(solution)/shard_map/dot_general | solution.py:17
  41.6 2.7 %collective-permute-start.12 = (f32[8,2176]{1,0:T(8,128)S(1)}, f32[8,2176]{1,0:T(8,128)S(1)}, u32[]{:S(2)}, u32[]{:S(2)}) collective-permute-start(f32[8,2176]{1,0:T(8,128)S(1)} %select_maximum_fusion.3), channel_id=1, source_target_pairs={{0,2},{1,3},{2,0},{3,1},{4,6},{5,7},{6,4},{7,5},{8,10},{9,11},{10,... | collective-permute-start | bytes 208904 | tf_op jit(solution)/shard_map/ppermute | solution.py:29
  46.4 2.7 %collective-permute-done.12 = f32[8,2176]{1,0:T(8,128)S(1)} collective-permute-done((f32[8,2176]{1,0:T(8,128)S(1)}, f32[8,2176]{1,0:T(8,128)S(1)}, u32[]{:S(2)}, u32[]{:S(2)}) %collective-permute-start.12) | collective-permute-done | bytes 69664 | tf_op jit(solution)/shard_map/ppermute | solution.py:29
  58.2 6.6 %collective-permute-done.15 = f32[32,2176]{1,0:T(8,128)S(1)} collective-permute-done((f32[32,2176]{1,0:T(8,128)S(1)}, f32[32,2176]{1,0:T(8,128)S(1)}, u32[]{:S(2)}, u32[]{:S(2)}) %collective-permute-start.15) | collective-permute-done | bytes 278560 | tf_op jit(solution)/shard_map/ppermute | solution.py:29
  67.0 5.7 %collective-permute-done.16 = f32[32,2176]{1,0:T(8,128)S(1)} collective-permute-done((f32[32,2176]{1,0:T(8,128)S(1)}, f32[32,2176]{1,0:T(8,128)S(1)}, u32[]{:S(2)}, u32[]{:S(2)}) %collective-permute-start.16) | collective-permute-done | bytes 278560 | tf_op jit(solution)/shard_map/ppermute | solution.py:29
  77.7 2.9 %fusion.4 = f32[128,2048]{1,0:T(8,128)S(1)} fusion(bf16[2048,2048]{1,0:T(8,128)(2,1)S(1)} %copy-done, f32[32,2048]{1,0:T(8,128)S(1)} %get-tuple-element.33, f32[32,2048]{1,0:T(8,128)S(1)} %get-tuple-element.31, f32[32,2048]{1,0:T(8,128)S(1)} %get-tuple-element.32, f32[32,2048]{1,0:T(8,128)S(1)} %get-tuple-element.30), kind=kOutput, calls=%fused_computation.15 | convolution fusion | flops 1075838976 | bytes 10485760 | tf_op jit(solution)/shard_map/dot_general | solution.py:17
  80.7 2.0 %collective-permute-start.24 = (f32[8,2176]{1,0:T(8,128)S(1)}, f32[8,2176]{1,0:T(8,128)S(1)}, u32[]{:S(2)}, u32[]{:S(2)}) collective-permute-start(f32[8,2176]{1,0:T(8,128)S(1)} %get-tuple-element.38), channel_id=1, source_target_pairs={{0,2},{1,3},{2,0},{3,1},{4,6},{5,7},{6,4},{7,5},{8,10},{9,11},{10,... | collective-permute-start | bytes 208904 | tf_op jit(solution)/shard_map/ppermute | solution.py:29
  83.7 3.9 %collective-permute-done.24 = f32[8,2176]{1,0:T(8,128)S(1)} collective-permute-done((f32[8,2176]{1,0:T(8,128)S(1)}, f32[8,2176]{1,0:T(8,128)S(1)}, u32[]{:S(2)}, u32[]{:S(2)}) %collective-permute-start.24) | collective-permute-done | bytes 69664 | tf_op jit(solution)/shard_map/ppermute | solution.py:29
  88.0 2.7 %collective-permute-start.23 = (f32[8,2176]{1,0:T(8,128)S(1)}, f32[8,2176]{1,0:T(8,128)S(1)}, u32[]{:S(2)}, u32[]{:S(2)}) collective-permute-start(f32[8,2176]{1,0:T(8,128)S(1)} %add.172), channel_id=1, source_target_pairs={{0,2},{1,3},{2,0},{3,1},{4,6},{5,7},{6,4},{7,5},{8,10},{9,11},{10,... | collective-permute-start | bytes 208904 | tf_op jit(solution)/shard_map/ppermute | solution.py:29
  90.7 1.8 %collective-permute-done.25 = f32[8,2176]{1,0:T(8,128)S(1)} collective-permute-done((f32[8,2176]{1,0:T(8,128)S(1)}, f32[8,2176]{1,0:T(8,128)S(1)}, u32[]{:S(2)}, u32[]{:S(2)}) %collective-permute-start.25) | collective-permute-done | bytes 69664 | tf_op jit(solution)/shard_map/ppermute | solution.py:29
  92.5 2.1 %collective-permute-done.23 = f32[8,2176]{1,0:T(8,128)S(1)} collective-permute-done((f32[8,2176]{1,0:T(8,128)S(1)}, f32[8,2176]{1,0:T(8,128)S(1)}, u32[]{:S(2)}, u32[]{:S(2)}) %collective-permute-start.23) | collective-permute-done | bytes 69664 | tf_op jit(solution)/shard_map/ppermute | solution.py:29
  102.2 6.4 %collective-permute-done.27 = f32[32,2176]{1,0:T(8,128)S(1)} collective-permute-done((f32[32,2176]{1,0:T(8,128)S(1)}, f32[32,2176]{1,0:T(8,128)S(1)}, u32[]{:S(2)}, u32[]{:S(2)}) %collective-permute-start.27) | collective-permute-done | bytes 278560 | tf_op jit(solution)/shard_map/ppermute | solution.py:29
  111.1 5.4 %collective-permute-done.28 = f32[32,2176]{1,0:T(8,128)S(1)} collective-permute-done((f32[32,2176]{1,0:T(8,128)S(1)}, f32[32,2176]{1,0:T(8,128)S(1)}, u32[]{:S(2)}, u32[]{:S(2)}) %collective-permute-start.28) | collective-permute-done | bytes 278560 | tf_op jit(solution)/shard_map/ppermute | solution.py:29
  120.3 2.9 %fusion.6 = f32[128,2048]{1,0:T(8,128)S(1)} fusion(bf16[2048,2048]{1,0:T(8,128)(2,1)S(1)} %copy-done, f32[32,2048]{1,0:T(8,128)S(1)} %get-tuple-element.29, f32[32,2048]{1,0:T(8,128)S(1)} %get-tuple-element.27, f32[32,2048]{1,0:T(8,128)S(1)} %get-tuple-element.28, f32[32,2048]{1,0:T(8,128)S(1)} %get-tuple-element.26), kind=kOutput, calls=%fused_computation.16 | convolution fusion | flops 1075838976 | bytes 10485760 | tf_op jit(solution)/shard_map/dot_general | solution.py:17
  125.1 5.1 %collective-permute-done.36 = f32[8,2176]{1,0:T(8,128)S(1)} collective-permute-done((f32[8,2176]{1,0:T(8,128)S(1)}, f32[8,2176]{1,0:T(8,128)S(1)}, u32[]{:S(2)}, u32[]{:S(2)}) %collective-permute-start.36) | collective-permute-done | bytes 69664 | tf_op jit(solution)/shard_map/ppermute | solution.py:29
  132.0 3.5 %collective-permute-done.37 = f32[8,2176]{1,0:T(8,128)S(1)} collective-permute-done((f32[8,2176]{1,0:T(8,128)S(1)}, f32[8,2176]{1,0:T(8,128)S(1)}, u32[]{:S(2)}, u32[]{:S(2)}) %collective-permute-start.37) | collective-permute-done | bytes 69664 | tf_op jit(solution)/shard_map/ppermute | solution.py:29
  144.8 6.5 %collective-permute-done.39 = f32[32,2176]{1,0:T(8,128)S(1)} collective-permute-done((f32[32,2176]{1,0:T(8,128)S(1)}, f32[32,2176]{1,0:T(8,128)S(1)}, u32[]{:S(2)}, u32[]{:S(2)}) %collective-permute-start.39) | collective-permute-done | bytes 278560 | tf_op jit(solution)/shard_map/ppermute | solution.py:29
  153.7 5.5 %collective-permute-done.40 = f32[32,2176]{1,0:T(8,128)S(1)} collective-permute-done((f32[32,2176]{1,0:T(8,128)S(1)}, f32[32,2176]{1,0:T(8,128)S(1)}, u32[]{:S(2)}, u32[]{:S(2)}) %collective-permute-start.40) | collective-permute-done | bytes 278560 | tf_op jit(solution)/shard_map/ppermute | solution.py:29
  163.4 2.9 %fusion.8 = f32[128,2048]{1,0:T(8,128)S(1)} fusion(bf16[2048,2048]{1,0:T(8,128)(2,1)S(1)} %copy-done, f32[128,2048]{1,0:T(8,128)S(1)} %pad_maximum_fusion.2), kind=kOutput, calls=%fused_computation.17 | convolution fusion | flops 1074003968 | bytes 10485760 | tf_op jit(solution)/shard_map/dot_general | solution.py:17
  166.4 1.9 %collective-permute-start.46 = (f32[8,2176]{1,0:T(8,128)S(1)}, f32[8,2176]{1,0:T(8,128)S(1)}, u32[]{:S(2)}, u32[]{:S(2)}) collective-permute-start(f32[8,2176]{1,0:T(8,128)S(1)} %get-tuple-element.35), channel_id=1, source_target_pairs={{0,1},{1,0},{2,3},{3,2},{4,5},{5,4},{6,7},{7,6},{8,9},{9,8},{10,11... | collective-permute-start | bytes 208904 | tf_op jit(solution)/shard_map/ppermute | solution.py:29
  168.3 4.7 %collective-permute-done.48 = f32[8,2176]{1,0:T(8,128)S(1)} collective-permute-done((f32[8,2176]{1,0:T(8,128)S(1)}, f32[8,2176]{1,0:T(8,128)S(1)}, u32[]{:S(2)}, u32[]{:S(2)}) %collective-permute-start.48) | collective-permute-done | bytes 69664 | tf_op jit(solution)/shard_map/ppermute | solution.py:29
  173.1 2.0 %collective-permute-start.47 = (f32[8,2176]{1,0:T(8,128)S(1)}, f32[8,2176]{1,0:T(8,128)S(1)}, u32[]{:S(2)}, u32[]{:S(2)}) collective-permute-start(f32[8,2176]{1,0:T(8,128)S(1)} %add.192), channel_id=1, source_target_pairs={{0,2},{1,3},{2,0},{3,1},{4,6},{5,7},{6,4},{7,5},{8,10},{9,11},{10,... | collective-permute-start | bytes 208904 | tf_op jit(solution)/shard_map/ppermute | solution.py:29
  175.1 3.4 %collective-permute-done.49 = f32[8,2176]{1,0:T(8,128)S(1)} collective-permute-done((f32[8,2176]{1,0:T(8,128)S(1)}, f32[8,2176]{1,0:T(8,128)S(1)}, u32[]{:S(2)}, u32[]{:S(2)}) %collective-permute-start.49) | collective-permute-done | bytes 69664 | tf_op jit(solution)/shard_map/ppermute | solution.py:29
  (199 shorter events, 70.1 us)
Async XLA Ops:
  8.1 6.4 %collective-permute-start.3 = (f32[8,2176]{1,0:T(8,128)S(1)}, f32[8,2176]{1,0:T(8,128)S(1)}, u32[]{:S(2)}, u32[]{:S(2)}) collective-permute-start(f32[8,2176]{1,0:T(8,128)S(1)} %fusion.77), channel_id=1, source_target_pairs={{0,24},{4,28},{8,16},{12,20},{16,8},{20,12},{24,0},{28,4},{1,25},{... | collective-permute-start | bytes 208904 | tf_op jit(solution)/shard_map/ppermute | solution.py:29
  19.5 7.2 %collective-permute-start.5 = (f32[8,2176]{1,0:T(8,128)S(1)}, f32[8,2176]{1,0:T(8,128)S(1)}, u32[]{:S(2)}, u32[]{:S(2)}) collective-permute-start(f32[8,2176]{1,0:T(8,128)S(1)} %select_maximum_fusion.5), channel_id=1, source_target_pairs={{0,2},{1,3},{2,0},{3,1},{4,6},{5,7},{6,4},{7,5},{8,10},{9,11},{10,... | collective-permute-start | bytes 208904 | tf_op jit(solution)/shard_map/ppermute | solution.py:29
  22.2 6.2 %collective-permute-start.6 = (f32[8,2176]{1,0:T(8,128)S(1)}, f32[8,2176]{1,0:T(8,128)S(1)}, u32[]{:S(2)}, u32[]{:S(2)}) collective-permute-start(f32[8,2176]{1,0:T(8,128)S(1)} %select_maximum_fusion.5), channel_id=1, source_target_pairs={{0,3},{1,2},{2,1},{3,0},{4,7},{5,6},{6,5},{7,4},{8,11},{9,10},{10,... | collective-permute-start | bytes 208904 | tf_op jit(solution)/shard_map/ppermute | solution.py:29
  23.5 5.1 %collective-permute-start.4 = (f32[8,2176]{1,0:T(8,128)S(1)}, f32[8,2176]{1,0:T(8,128)S(1)}, u32[]{:S(2)}, u32[]{:S(2)}) collective-permute-start(f32[8,2176]{1,0:T(8,128)S(1)} %select_maximum_fusion.5), channel_id=1, source_target_pairs={{0,1},{1,0},{2,3},{3,2},{4,5},{5,4},{6,7},{7,6},{8,9},{9,8},{10,11... | collective-permute-start | bytes 208904 | tf_op jit(solution)/shard_map/ppermute | solution.py:29
  31.6 5.3 %collective-permute-start.10 = (f32[8,2176]{1,0:T(8,128)S(1)}, f32[8,2176]{1,0:T(8,128)S(1)}, u32[]{:S(2)}, u32[]{:S(2)}) collective-permute-start(f32[8,2176]{1,0:T(8,128)S(1)} %fusion.78), channel_id=1, source_target_pairs={{0,24},{4,28},{8,16},{12,20},{16,8},{20,12},{24,0},{28,4},{1,25},{... | collective-permute-start | bytes 208904 | tf_op jit(solution)/shard_map/ppermute | solution.py:29
  33.2 5.1 %collective-permute-start.9 = (f32[8,2176]{1,0:T(8,128)S(1)}, f32[8,2176]{1,0:T(8,128)S(1)}, u32[]{:S(2)}, u32[]{:S(2)}) collective-permute-start(f32[8,2176]{1,0:T(8,128)S(1)} %fusion.78), channel_id=1, source_target_pairs={{0,16},{4,20},{8,24},{12,28},{16,0},{20,4},{24,8},{28,12},{1,17},{... | collective-permute-start | bytes 208904 | tf_op jit(solution)/shard_map/ppermute | solution.py:29
  41.6 7.5 %collective-permute-start.12 = (f32[8,2176]{1,0:T(8,128)S(1)}, f32[8,2176]{1,0:T(8,128)S(1)}, u32[]{:S(2)}, u32[]{:S(2)}) collective-permute-start(f32[8,2176]{1,0:T(8,128)S(1)} %select_maximum_fusion.3), channel_id=1, source_target_pairs={{0,2},{1,3},{2,0},{3,1},{4,6},{5,7},{6,4},{7,5},{8,10},{9,11},{10,... | collective-permute-start | bytes 208904 | tf_op jit(solution)/shard_map/ppermute | solution.py:29
  44.3 6.2 %collective-permute-start.13 = (f32[8,2176]{1,0:T(8,128)S(1)}, f32[8,2176]{1,0:T(8,128)S(1)}, u32[]{:S(2)}, u32[]{:S(2)}) collective-permute-start(f32[8,2176]{1,0:T(8,128)S(1)} %select_maximum_fusion.3), channel_id=1, source_target_pairs={{0,3},{1,2},{2,1},{3,0},{4,7},{5,6},{6,5},{7,4},{8,11},{9,10},{10,... | collective-permute-start | bytes 208904 | tf_op jit(solution)/shard_map/ppermute | solution.py:29
  44.8 5.7 %collective-permute-start.11 = (f32[8,2176]{1,0:T(8,128)S(1)}, f32[8,2176]{1,0:T(8,128)S(1)}, u32[]{:S(2)}, u32[]{:S(2)}) collective-permute-start(f32[8,2176]{1,0:T(8,128)S(1)} %select_maximum_fusion.3), channel_id=1, source_target_pairs={{0,1},{1,0},{2,3},{3,2},{4,5},{5,4},{6,7},{7,6},{8,9},{9,8},{10,11... | collective-permute-start | bytes 208904 | tf_op jit(solution)/shard_map/ppermute | solution.py:29
  56.0 8.8 %collective-permute-start.15 = (f32[32,2176]{1,0:T(8,128)S(1)}, f32[32,2176]{1,0:T(8,128)S(1)}, u32[]{:S(2)}, u32[]{:S(2)}) collective-permute-start(f32[32,2176]{1,0:T(8,128)S(1)} %get-tuple-element.16), channel_id=1, source_target_pairs={{0,8},{4,12},{8,0},{12,4},{16,24},{20,28},{24,16},{28,20},{1,9},{5... | collective-permute-start | bytes 835592 | tf_op jit(solution)/shard_map/ppermute | solution.py:29
  57.5 8.8 %collective-permute-start.19 = (f32[32,2176]{1,0:T(8,128)S(1)}, f32[32,2176]{1,0:T(8,128)S(1)}, u32[]{:S(2)}, u32[]{:S(2)}) collective-permute-start(f32[32,2176]{1,0:T(8,128)S(1)} %get-tuple-element.17), channel_id=1, source_target_pairs={{0,16},{4,20},{8,24},{12,28},{16,0},{20,4},{24,8},{28,12},{1,17},{... | collective-permute-start | bytes 835592 | tf_op jit(solution)/shard_map/ppermute | solution.py:29
  64.8 7.9 %collective-permute-start.16 = (f32[32,2176]{1,0:T(8,128)S(1)}, f32[32,2176]{1,0:T(8,128)S(1)}, u32[]{:S(2)}, u32[]{:S(2)}) collective-permute-start(f32[32,2176]{1,0:T(8,128)S(1)} %add.167), channel_id=1, source_target_pairs={{0,16},{4,20},{8,24},{12,28},{16,0},{20,4},{24,8},{28,12},{1,17},{... | collective-permute-start | bytes 835592 | tf_op jit(solution)/shard_map/ppermute | solution.py:29
  66.3 7.6 %collective-permute-start.20 = (f32[32,2176]{1,0:T(8,128)S(1)}, f32[32,2176]{1,0:T(8,128)S(1)}, u32[]{:S(2)}, u32[]{:S(2)}) collective-permute-start(f32[32,2176]{1,0:T(8,128)S(1)} %add.170), channel_id=1, source_target_pairs={{0,8},{4,12},{8,0},{12,4},{16,24},{20,28},{24,16},{28,20},{1,9},{5... | collective-permute-start | bytes 835592 | tf_op jit(solution)/shard_map/ppermute | solution.py:29
  80.7 7.0 %collective-permute-start.24 = (f32[8,2176]{1,0:T(8,128)S(1)}, f32[8,2176]{1,0:T(8,128)S(1)}, u32[]{:S(2)}, u32[]{:S(2)}) collective-permute-start(f32[8,2176]{1,0:T(8,128)S(1)} %get-tuple-element.38), channel_id=1, source_target_pairs={{0,2},{1,3},{2,0},{3,1},{4,6},{5,7},{6,4},{7,5},{8,10},{9,11},{10,... | collective-permute-start | bytes 208904 | tf_op jit(solution)/shard_map/ppermute | solution.py:29
  82.7 5.3 %collective-permute-start.22 = (f32[8,2176]{1,0:T(8,128)S(1)}, f32[8,2176]{1,0:T(8,128)S(1)}, u32[]{:S(2)}, u32[]{:S(2)}) collective-permute-start(f32[8,2176]{1,0:T(8,128)S(1)} %get-tuple-element.39), channel_id=1, source_target_pairs={{0,1},{1,0},{2,3},{3,2},{4,5},{5,4},{6,7},{7,6},{8,9},{9,8},{10,11... | collective-permute-start | bytes 208904 | tf_op jit(solution)/shard_map/ppermute | solution.py:29
  88.0 6.6 %collective-permute-start.23 = (f32[8,2176]{1,0:T(8,128)S(1)}, f32[8,2176]{1,0:T(8,128)S(1)}, u32[]{:S(2)}, u32[]{:S(2)}) collective-permute-start(f32[8,2176]{1,0:T(8,128)S(1)} %add.172), channel_id=1, source_target_pairs={{0,2},{1,3},{2,0},{3,1},{4,6},{5,7},{6,4},{7,5},{8,10},{9,11},{10,... | collective-permute-start | bytes 208904 | tf_op jit(solution)/shard_map/ppermute | solution.py:29
  99.8 8.8 %collective-permute-start.27 = (f32[32,2176]{1,0:T(8,128)S(1)}, f32[32,2176]{1,0:T(8,128)S(1)}, u32[]{:S(2)}, u32[]{:S(2)}) collective-permute-start(f32[32,2176]{1,0:T(8,128)S(1)} %get-tuple-element.12), channel_id=1, source_target_pairs={{0,8},{4,12},{8,0},{12,4},{16,24},{20,28},{24,16},{28,20},{1,9},{5... | collective-permute-start | bytes 835592 | tf_op jit(solution)/shard_map/ppermute | solution.py:29
  100.5 9.0 %collective-permute-start.31 = (f32[32,2176]{1,0:T(8,128)S(1)}, f32[32,2176]{1,0:T(8,128)S(1)}, u32[]{:S(2)}, u32[]{:S(2)}) collective-permute-start(f32[32,2176]{1,0:T(8,128)S(1)} %get-tuple-element.13), channel_id=1, source_target_pairs={{0,16},{4,20},{8,24},{12,28},{16,0},{20,4},{24,8},{28,12},{1,17},{... | collective-permute-start | bytes 835592 | tf_op jit(solution)/shard_map/ppermute | solution.py:29
  108.6 7.9 %collective-permute-start.28 = (f32[32,2176]{1,0:T(8,128)S(1)}, f32[32,2176]{1,0:T(8,128)S(1)}, u32[]{:S(2)}, u32[]{:S(2)}) collective-permute-start(f32[32,2176]{1,0:T(8,128)S(1)} %add.177), channel_id=1, source_target_pairs={{0,16},{4,20},{8,24},{12,28},{16,0},{20,4},{24,8},{28,12},{1,17},{... | collective-permute-start | bytes 835592 | tf_op jit(solution)/shard_map/ppermute | solution.py:29
  109.6 7.6 %collective-permute-start.32 = (f32[32,2176]{1,0:T(8,128)S(1)}, f32[32,2176]{1,0:T(8,128)S(1)}, u32[]{:S(2)}, u32[]{:S(2)}) collective-permute-start(f32[32,2176]{1,0:T(8,128)S(1)} %add.180), channel_id=1, source_target_pairs={{0,8},{4,12},{8,0},{12,4},{16,24},{20,28},{24,16},{28,20},{1,9},{5... | collective-permute-start | bytes 835592 | tf_op jit(solution)/shard_map/ppermute | solution.py:29
  123.3 6.9 %collective-permute-start.36 = (f32[8,2176]{1,0:T(8,128)S(1)}, f32[8,2176]{1,0:T(8,128)S(1)}, u32[]{:S(2)}, u32[]{:S(2)}) collective-permute-start(f32[8,2176]{1,0:T(8,128)S(1)} %get-tuple-element.36), channel_id=1, source_target_pairs={{0,2},{1,3},{2,0},{3,1},{4,6},{5,7},{6,4},{7,5},{8,10},{9,11},{10,... | collective-permute-start | bytes 208904 | tf_op jit(solution)/shard_map/ppermute | solution.py:29
  124.6 5.7 %collective-permute-start.34 = (f32[8,2176]{1,0:T(8,128)S(1)}, f32[8,2176]{1,0:T(8,128)S(1)}, u32[]{:S(2)}, u32[]{:S(2)}) collective-permute-start(f32[8,2176]{1,0:T(8,128)S(1)} %get-tuple-element.37), channel_id=1, source_target_pairs={{0,1},{1,0},{2,3},{3,2},{4,5},{5,4},{6,7},{7,6},{8,9},{9,8},{10,11... | collective-permute-start | bytes 208904 | tf_op jit(solution)/shard_map/ppermute | solution.py:29
  130.2 5.4 %collective-permute-start.37 = (f32[8,2176]{1,0:T(8,128)S(1)}, f32[8,2176]{1,0:T(8,128)S(1)}, u32[]{:S(2)}, u32[]{:S(2)}) collective-permute-start(f32[8,2176]{1,0:T(8,128)S(1)} %add.184), channel_id=1, source_target_pairs={{0,1},{1,0},{2,3},{3,2},{4,5},{5,4},{6,7},{7,6},{8,9},{9,8},{10,11... | collective-permute-start | bytes 208904 | tf_op jit(solution)/shard_map/ppermute | solution.py:29
  130.3 6.8 %collective-permute-start.35 = (f32[8,2176]{1,0:T(8,128)S(1)}, f32[8,2176]{1,0:T(8,128)S(1)}, u32[]{:S(2)}, u32[]{:S(2)}) collective-permute-start(f32[8,2176]{1,0:T(8,128)S(1)} %add.182), channel_id=1, source_target_pairs={{0,2},{1,3},{2,0},{3,1},{4,6},{5,7},{6,4},{7,5},{8,10},{9,11},{10,... | collective-permute-start | bytes 208904 | tf_op jit(solution)/shard_map/ppermute | solution.py:29
  142.6 8.8 %collective-permute-start.39 = (f32[32,2176]{1,0:T(8,128)S(1)}, f32[32,2176]{1,0:T(8,128)S(1)}, u32[]{:S(2)}, u32[]{:S(2)}) collective-permute-start(f32[32,2176]{1,0:T(8,128)S(1)} %get-tuple-element.8), channel_id=1, source_target_pairs={{0,8},{4,12},{8,0},{12,4},{16,24},{20,28},{24,16},{28,20},{1,9},{5... | collective-permute-start | bytes 835592 | tf_op jit(solution)/shard_map/ppermute | solution.py:29
  143.7 8.8 %collective-permute-start.43 = (f32[32,2176]{1,0:T(8,128)S(1)}, f32[32,2176]{1,0:T(8,128)S(1)}, u32[]{:S(2)}, u32[]{:S(2)}) collective-permute-start(f32[32,2176]{1,0:T(8,128)S(1)} %get-tuple-element.9), channel_id=1, source_target_pairs={{0,16},{4,20},{8,24},{12,28},{16,0},{20,4},{24,8},{28,12},{1,17},{... | collective-permute-start | bytes 835592 | tf_op jit(solution)/shard_map/ppermute | solution.py:29
  151.4 7.9 %collective-permute-start.40 = (f32[32,2176]{1,0:T(8,128)S(1)}, f32[32,2176]{1,0:T(8,128)S(1)}, u32[]{:S(2)}, u32[]{:S(2)}) collective-permute-start(f32[32,2176]{1,0:T(8,128)S(1)} %add.187), channel_id=1, source_target_pairs={{0,16},{4,20},{8,24},{12,28},{16,0},{20,4},{24,8},{28,12},{1,17},{... | collective-permute-start | bytes 835592 | tf_op jit(solution)/shard_map/ppermute | solution.py:29
  152.5 7.6 %collective-permute-start.44 = (f32[32,2176]{1,0:T(8,128)S(1)}, f32[32,2176]{1,0:T(8,128)S(1)}, u32[]{:S(2)}, u32[]{:S(2)}) collective-permute-start(f32[32,2176]{1,0:T(8,128)S(1)} %add.190), channel_id=1, source_target_pairs={{0,8},{4,12},{8,0},{12,4},{16,24},{20,28},{24,16},{28,20},{1,9},{5... | collective-permute-start | bytes 835592 | tf_op jit(solution)/shard_map/ppermute | solution.py:29
  166.4 6.6 %collective-permute-start.48 = (f32[8,2176]{1,0:T(8,128)S(1)}, f32[8,2176]{1,0:T(8,128)S(1)}, u32[]{:S(2)}, u32[]{:S(2)}) collective-permute-start(f32[8,2176]{1,0:T(8,128)S(1)} %get-tuple-element.34), channel_id=1, source_target_pairs={{0,2},{1,3},{2,0},{3,1},{4,6},{5,7},{6,4},{7,5},{8,10},{9,11},{10,... | collective-permute-start | bytes 208904 | tf_op jit(solution)/shard_map/ppermute | solution.py:29
  166.4 6.7 %collective-permute-start.46 = (f32[8,2176]{1,0:T(8,128)S(1)}, f32[8,2176]{1,0:T(8,128)S(1)}, u32[]{:S(2)}, u32[]{:S(2)}) collective-permute-start(f32[8,2176]{1,0:T(8,128)S(1)} %get-tuple-element.35), channel_id=1, source_target_pairs={{0,1},{1,0},{2,3},{3,2},{4,5},{5,4},{6,7},{7,6},{8,9},{9,8},{10,11... | collective-permute-start | bytes 208904 | tf_op jit(solution)/shard_map/ppermute | solution.py:29
  173.0 5.4 %collective-permute-start.49 = (f32[8,2176]{1,0:T(8,128)S(1)}, f32[8,2176]{1,0:T(8,128)S(1)}, u32[]{:S(2)}, u32[]{:S(2)}) collective-permute-start(f32[8,2176]{1,0:T(8,128)S(1)} %add.194), channel_id=1, source_target_pairs={{0,1},{1,0},{2,3},{3,2},{4,5},{5,4},{6,7},{7,6},{8,9},{9,8},{10,11... | collective-permute-start | bytes 208904 | tf_op jit(solution)/shard_map/ppermute | solution.py:29
  173.1 6.8 %collective-permute-start.47 = (f32[8,2176]{1,0:T(8,128)S(1)}, f32[8,2176]{1,0:T(8,128)S(1)}, u32[]{:S(2)}, u32[]{:S(2)}) collective-permute-start(f32[8,2176]{1,0:T(8,128)S(1)} %add.192), channel_id=1, source_target_pairs={{0,2},{1,3},{2,0},{3,1},{4,6},{5,7},{6,4},{7,5},{8,10},{9,11},{10,... | collective-permute-start | bytes 208904 | tf_op jit(solution)/shard_map/ppermute | solution.py:29
  (26 other events, 174.0 us)

commit v3 on v2

--- a/solution.py
+++ b/solution.py
@@ -10,7 +10,7 @@
 LANES = 128
 TOTAL = CHILDREN * K_CHILD
 
-HIGH = lax.Precision.HIGHEST
+HIGH = lax.Precision.HIGH
 
 
 def times_transpose(left_bf, matrix):
@@ -45,13 +45,13 @@
     return x
 
 
-def crossing(first, second, axis, size, masks):
-    for a, b in zip(masks, masks[::-1]):
-        first, second = (
-            first + swap(first, axis, size, a),
-            second + swap(second, axis, size, b),
-        )
-    return first, second
+def crossing(parts, axis, size, masks):
+    parts = list(parts)
+    orders = [masks, masks[::-1]]
+    for step in range(len(masks)):
+        for i in range(len(parts)):
+            parts[i] = parts[i] + swap(parts[i], axis, size, orders[i % 2][step])
+    return parts
 
 
 def pad_lanes(x):
@@ -94,9 +94,10 @@
         )
         child_w = child_rows * jnp.sum(member * root_w, axis=0)[None, :]
         child_h = child_cols * jnp.repeat(root_h, K_CHILD, axis=0)
-        quarter = TOTAL // 4
-        pieces = [child_h[i * quarter : (i + 1) * quarter] for i in range(4)]
-        mine = [jnp.where(is_odd, pieces[i + 2], pieces[i]) for i in range(2)]
+        parts_each = CHILDREN // 2
+        size = TOTAL // CHILDREN
+        pieces = [child_h[i * size : (i + 1) * size] for i in range(CHILDREN)]
+        mine = [jnp.where(is_odd, pieces[i + parts_each], pieces[i]) for i in range(parts_each)]
         same = (
             jnp.arange(TOTAL, dtype=jnp.int32)[None, :] // K_CHILD
             == jnp.arange(CHILDREN, dtype=jnp.int32)[:, None]
@@ -106,30 +107,30 @@
             gram = outer(spread, child_w)
             numer = jnp.dot(spread.astype(jnp.bfloat16), matrix, preferred_element_type=jnp.float32)
             packed = jnp.concatenate([numer, pad_lanes(gram)], axis=1)
-            pieces = [packed[i * quarter : (i + 1) * quarter] for i in range(4)]
+            pieces = [packed[i * size : (i + 1) * size] for i in range(CHILDREN)]
             parts = []
-            for i in range(2):
-                keep = jnp.where(is_odd, pieces[i + 2], pieces[i])
-                send = jnp.where(is_odd, pieces[i], pieces[i + 2])
+            for i in range(parts_each):
+                keep = jnp.where(is_odd, pieces[i + parts_each], pieces[i])
+                send = jnp.where(is_odd, pieces[i], pieces[i + parts_each])
                 parts.append(keep + swap(send, "row", rows, 1))
-            parts = crossing(*parts, "row", rows, row_masks[1:])
+            parts = crossing(parts, "row", rows, row_masks[1:])
             low, high = [], []
-            for i in range(2):
-                gram = parts[i][:, bins : bins + K_CHILD].reshape(-1, K_CHILD, K_CHILD)
-                blocks = mine[i].reshape(-1, K_CHILD, bins)
-                lower = jnp.einsum("cjk,ckn->cjn", gram, blocks, precision=HIGH).reshape(quarter, bins)
+            for i in range(parts_each):
+                gram = parts[i][:, bins : bins + K_CHILD]
+                lower = jnp.dot(gram, mine[i], precision=HIGH)
                 mine[i] = mine[i] * parts[i][:, :bins] / lower
-                other = swap(mine[i], "row", rows, 1)
-                low.append(jnp.where(is_odd, other, mine[i]))
-                high.append(jnp.where(is_odd, mine[i], other))
-            child_h = jnp.concatenate(low + high)
-            full = outer(child_h, child_h).reshape(CHILDREN, K_CHILD, TOTAL)
-            gram = jnp.sum(full * same[:, None, :], axis=0)
+                tiled = jnp.concatenate([mine[i]] * CHILDREN)
+                packed = jnp.concatenate([mine[i], outer(mine[i], tiled)], axis=1)
+                other = swap(packed, "row", rows, 1)
+                low.append(jnp.where(is_odd, other, packed))
+                high.append(jnp.where(is_odd, packed, other))
+            child_h = jnp.concatenate([x[:, :bins] for x in low + high])
+            gram = sum(x[:, bins:] * same[c : c + 1] for c, x in enumerate(low + high))
             numer = times_transpose(child_h.astype(jnp.bfloat16), matrix)
             numer = jnp.sum(numer.reshape(CHILDREN, K_CHILD, nodes) * member[:, None, :], axis=0)
             packed = jnp.concatenate([numer, gram], axis=1)
             half = K_CHILD // 2
-            packed = jnp.concatenate(crossing(packed[:half], packed[half:], "col", cols, col_masks))
+            packed = jnp.concatenate(crossing([packed[:half], packed[half:]], "col", cols, col_masks))
             lower = jnp.dot(packed[:, nodes:], spread, precision=HIGH)
             child_w = child_w * packed[:, :nodes] / lower
         return (root_w, root_h, child_w, child_h)

time: 181 us -> 171 us (0.945)
  waiting for transfers between devices: 92.3 us -> 63.2 us
  starting transfers between devices: 46.5 us -> 61.2 us
    ppermute x50 -> x74, waiting for transfers between devices: 92.3 us -> 63.2 us  [swap(): return lax.ppermute(x, axis, [(i, i ^ mask) for i in range(size)])]
    ppermute x50 -> x74, starting transfers between devices: 46.5 us -> 61.2 us  [swap(): return lax.ppermute(x, axis, [(i, i ^ mask) for i in range(size)])]
    dot_general x10 -> x19, matrix products: 7.5 us -> 9.31 us  [outer(): lax.dot_general(a, b, (((1,), (1,)), ((), ())), precision=HIGH, preferred...]
  transfers between devices with their start and end apart: 50 -> 74, of which waited for: 45 -> 54; matrix products, arithmetic and copies ran while one was open for 2% -> 7% of each run, Pallas kernels for 0% -> 0%
where the time goes in v3:
time: 171 us; the launch traced here: 170 us
  waiting for transfers between devices  63.2 us (37%)
  starting transfers between devices  61.2 us (36%)
  matrix products  38.3 us (22%)
  between operations  3.13 us (2%)
  other arithmetic  2.86 us (2%)
  local copies, waits for them, and re-layouts  1.78 us (1%)
    ppermute x74, waiting for transfers between devices, swap(): return lax.ppermute(x, axis, [(i, i ^ mask) for i in range(size)])  63.2 us
    ppermute x74, starting transfers between devices, swap(): return lax.ppermute(x, axis, [(i, i ^ mask) for i in range(size)])  61.2 us
    dot_general x5, matrix products, times_transpose(): lax.dot_general(left_bf, matrix, (((1,), (1,)), ((), ())), preferred_elem...  13.5 us
    dot_general x19, matrix products, outer(): lax.dot_general(a, b, (((1,), (1,)), ((), ())), precision=HIGH, preferred...  9.31 us
    dot_general x2, matrix products, body(): jnp.dot(root_w.astype(jnp.bfloat16), matrix, preferred_element_type=jnp.f...  6.07 us
    dot_general x3, matrix products, body(): jnp.dot(spread.astype(jnp.bfloat16), matrix, preferred_element_type=jnp.f...  3.87 us
  transfers between devices with their start and end apart: 74, of which 54 were waited for; matrix products, arithmetic and copies ran while one was open for 7% of the time, Pallas kernels for 0%

profile of v3, /device:TPU:0, one launch (start us, length us, event | category | flops | bytes accessed | tf_op | source)
XLA Modules:
  0.0 170.5 jit_solution(10144613114500908074)
XLA Ops:
  1.7 4.8 %fusion.47 = f32[8,2048]{1,0:T(8,128)S(1)} fusion(bf16[2048,2048]{1,0:T(8,128)(2,1)} %param.6, f32[8,2048]{1,0:T(8,128)} %param.8), kind=kOutput, calls=%fused_computation.301 | convolution fusion | flops 67125248 | bytes 8519680 | tf_op jit(solution)/shard_map/dot_general | solution.py:85
  8.0 2.9 %collective-permute-start.2 = (f32[8,2176]{1,0:T(8,128)S(1)}, f32[8,2176]{1,0:T(8,128)S(1)}, u32[]{:S(2)}, u32[]{:S(2)}) collective-permute-start(f32[8,2176]{1,0:T(8,128)S(1)} %fusion.132), channel_id=1, source_target_pairs={{0,16},{4,20},{8,24},{12,28},{16,0},{20,4},{24,8},{28,12},{1,17},{... | collective-permute-start | bytes 208904 | tf_op jit(solution)/shard_map/ppermute | solution.py:29
  12.5 1.8 %collective-permute-done.2 = f32[8,2176]{1,0:T(8,128)S(1)} collective-permute-done((f32[8,2176]{1,0:T(8,128)S(1)}, f32[8,2176]{1,0:T(8,128)S(1)}, u32[]{:S(2)}, u32[]{:S(2)}) %collective-permute-start.2) | collective-permute-done | bytes 69664 | tf_op jit(solution)/shard_map/ppermute | solution.py:29
  14.3 2.5 %collective-permute-done.3 = f32[8,2176]{1,0:T(8,128)S(1)} collective-permute-done((f32[8,2176]{1,0:T(8,128)S(1)}, f32[8,2176]{1,0:T(8,128)S(1)}, u32[]{:S(2)}, u32[]{:S(2)}) %collective-permute-start.3) | collective-permute-done | bytes 69664 | tf_op jit(solution)/shard_map/ppermute | solution.py:29
  17.1 2.3 %fusion.45 = f32[8,2048]{1,0:T(8,128)S(1)} fusion(bf16[2048,2048]{1,0:T(8,128)(2,1)S(1)} %copy-done, f32[8,2048]{1,0:T(8,128)S(1)} %fusion.35), kind=kOutput, calls=%fused_computation.299 | convolution fusion | flops 67125248 | bytes 8519680 | tf_op jit(solution)/shard_map/dot_general | solution.py:17
  19.4 2.7 %collective-permute-start.5 = (f32[8,2176]{1,0:T(8,128)S(1)}, f32[8,2176]{1,0:T(8,128)S(1)}, u32[]{:S(2)}, u32[]{:S(2)}) collective-permute-start(f32[8,2176]{1,0:T(8,128)S(1)} %select_maximum_fusion.5), channel_id=1, source_target_pairs={{0,2},{1,3},{2,0},{3,1},{4,6},{5,7},{6,4},{7,5},{8,10},{9,11},{10,... | collective-permute-start | bytes 208904 | tf_op jit(solution)/shard_map/ppermute | solution.py:29
  24.8 3.4 %collective-permute-done.6 = f32[8,2176]{1,0:T(8,128)S(1)} collective-permute-done((f32[8,2176]{1,0:T(8,128)S(1)}, f32[8,2176]{1,0:T(8,128)S(1)}, u32[]{:S(2)}, u32[]{:S(2)}) %collective-permute-start.6) | collective-permute-done | bytes 69664 | tf_op jit(solution)/shard_map/ppermute | solution.py:29
  35.8 2.8 %collective-permute-done.10 = f32[8,2176]{1,0:T(8,128)S(1)} collective-permute-done((f32[8,2176]{1,0:T(8,128)S(1)}, f32[8,2176]{1,0:T(8,128)S(1)}, u32[]{:S(2)}, u32[]{:S(2)}) %collective-permute-start.10) | collective-permute-done | bytes 69664 | tf_op jit(solution)/shard_map/ppermute | solution.py:29
  39.0 2.3 %fusion.41 = f32[8,2048]{1,0:T(8,128)S(1)} fusion(bf16[2048,2048]{1,0:T(8,128)(2,1)S(1)} %copy-done, f32[8,2048]{1,0:T(8,128)S(1)} %fusion.33), kind=kOutput, calls=%fused_computation.295 | convolution fusion | flops 67125248 | bytes 8519680 | tf_op jit(solution)/shard_map/dot_general | solution.py:17
  41.3 2.2 %collective-permute-start.12 = (f32[8,2176]{1,0:T(8,128)S(1)}, f32[8,2176]{1,0:T(8,128)S(1)}, u32[]{:S(2)}, u32[]{:S(2)}) collective-permute-start(f32[8,2176]{1,0:T(8,128)S(1)} %select_maximum_fusion.3), channel_id=1, source_target_pairs={{0,2},{1,3},{2,0},{3,1},{4,6},{5,7},{6,4},{7,5},{8,10},{9,11},{10,... | collective-permute-start | bytes 208904 | tf_op jit(solution)/shard_map/ppermute | solution.py:29
  46.0 2.5 %collective-permute-done.12 = f32[8,2176]{1,0:T(8,128)S(1)} collective-permute-done((f32[8,2176]{1,0:T(8,128)S(1)}, f32[8,2176]{1,0:T(8,128)S(1)}, u32[]{:S(2)}, u32[]{:S(2)}) %collective-permute-start.12) | collective-permute-done | bytes 69664 | tf_op jit(solution)/shard_map/ppermute | solution.py:29
  59.1 2.5 %collective-permute-done.27 = f32[16,2176]{1,0:T(8,128)S(1)} collective-permute-done((f32[16,2176]{1,0:T(8,128)S(1)}, f32[16,2176]{1,0:T(8,128)S(1)}, u32[]{:S(2)}, u32[]{:S(2)}) %collective-permute-start.27) | collective-permute-done | bytes 139296 | tf_op jit(solution)/shard_map/ppermute | solution.py:29
  66.7 2.2 %collective-permute-done.28 = f32[16,2176]{1,0:T(8,128)S(1)} collective-permute-done((f32[16,2176]{1,0:T(8,128)S(1)}, f32[16,2176]{1,0:T(8,128)S(1)}, u32[]{:S(2)}, u32[]{:S(2)}) %collective-permute-start.28) | collective-permute-done | bytes 139296 | tf_op jit(solution)/shard_map/ppermute | solution.py:29
  75.3 2.9 %fusion.143 = f32[128,2048]{1,0:T(8,128)S(1)} fusion(bf16[128,2048]{1,0:T(8,128)(2,1)S(1)} %constant_dynamic-update-slice_fusion.32, bf16[2048,2048]{1,0:T(8,128)(2,1)S(1)} %copy-done), kind=kOutput, calls=%fused_computation.413 | convolution fusion | flops 1073741824 | bytes 9961472 | tf_op jit(solution)/shard_map/dot_general | solution.py:17
  79.1 2.0 %collective-permute-start.32 = (f32[8,2176]{1,0:T(8,128)S(1)}, f32[8,2176]{1,0:T(8,128)S(1)}, u32[]{:S(2)}, u32[]{:S(2)}) collective-permute-start(f32[8,2176]{1,0:T(8,128)S(1)} %get-tuple-element.60), channel_id=1, source_target_pairs={{0,2},{1,3},{2,0},{3,1},{4,6},{5,7},{6,4},{7,5},{8,10},{9,11},{10,... | collective-permute-start | bytes 208904 | tf_op jit(solution)/shard_map/ppermute | solution.py:29
  81.1 2.5 %collective-permute-done.30 = f32[8,2176]{1,0:T(8,128)S(1)} collective-permute-done((f32[8,2176]{1,0:T(8,128)S(1)}, f32[8,2176]{1,0:T(8,128)S(1)}, u32[]{:S(2)}, u32[]{:S(2)}) %collective-permute-start.30) | collective-permute-done | bytes 69664 | tf_op jit(solution)/shard_map/ppermute | solution.py:29
  85.9 3.4 %collective-permute-done.31 = f32[8,2176]{1,0:T(8,128)S(1)} collective-permute-done((f32[8,2176]{1,0:T(8,128)S(1)}, f32[8,2176]{1,0:T(8,128)S(1)}, u32[]{:S(2)}, u32[]{:S(2)}) %collective-permute-start.31) | collective-permute-done | bytes 69664 | tf_op jit(solution)/shard_map/ppermute | solution.py:29
  99.0 2.5 %collective-permute-done.47 = f32[16,2176]{1,0:T(8,128)S(1)} collective-permute-done((f32[16,2176]{1,0:T(8,128)S(1)}, f32[16,2176]{1,0:T(8,128)S(1)}, u32[]{:S(2)}, u32[]{:S(2)}) %collective-permute-start.47) | collective-permute-done | bytes 139296 | tf_op jit(solution)/shard_map/ppermute | solution.py:29
  106.6 1.6 collective-permute-done.48
  114.4 3.1 %fusion.149 = f32[128,2048]{1,0:T(8,128)S(1)} fusion(bf16[128,2048]{1,0:T(8,128)(2,1)S(1)} %constant_dynamic-update-slice_fusion.72, bf16[2048,2048]{1,0:T(8,128)(2,1)S(1)} %copy-done), kind=kOutput, calls=%fused_computation.419 | convolution fusion | flops 1073741824 | bytes 9961472 | tf_op jit(solution)/shard_map/dot_general | solution.py:17
  117.8 2.5 %collective-permute-start.52 = (f32[8,2176]{1,0:T(8,128)S(1)}, f32[8,2176]{1,0:T(8,128)S(1)}, u32[]{:S(2)}, u32[]{:S(2)}) collective-permute-start(f32[8,2176]{1,0:T(8,128)S(1)} %get-tuple-element.58), channel_id=1, source_target_pairs={{0,2},{1,3},{2,0},{3,1},{4,6},{5,7},{6,4},{7,5},{8,10},{9,11},{10,... | collective-permute-start | bytes 208904 | tf_op jit(solution)/shard_map/ppermute | solution.py:29
  120.4 2.9 %collective-permute-done.50 = f32[8,2176]{1,0:T(8,128)S(1)} collective-permute-done((f32[8,2176]{1,0:T(8,128)S(1)}, f32[8,2176]{1,0:T(8,128)S(1)}, u32[]{:S(2)}, u32[]{:S(2)}) %collective-permute-start.50) | collective-permute-done | bytes 69664 | tf_op jit(solution)/shard_map/ppermute | solution.py:29
  124.7 1.5 collective-permute-start.53
  126.2 2.9 %collective-permute-done.51 = f32[8,2176]{1,0:T(8,128)S(1)} collective-permute-done((f32[8,2176]{1,0:T(8,128)S(1)}, f32[8,2176]{1,0:T(8,128)S(1)}, u32[]{:S(2)}, u32[]{:S(2)}) %collective-permute-start.51) | collective-permute-done | bytes 69664 | tf_op jit(solution)/shard_map/ppermute | solution.py:29
  138.5 2.5 %collective-permute-done.67 = f32[16,2176]{1,0:T(8,128)S(1)} collective-permute-done((f32[16,2176]{1,0:T(8,128)S(1)}, f32[16,2176]{1,0:T(8,128)S(1)}, u32[]{:S(2)}, u32[]{:S(2)}) %collective-permute-start.67) | collective-permute-done | bytes 139296 | tf_op jit(solution)/shard_map/ppermute | solution.py:29
  146.1 2.2 %collective-permute-done.68 = f32[16,2176]{1,0:T(8,128)S(1)} collective-permute-done((f32[16,2176]{1,0:T(8,128)S(1)}, f32[16,2176]{1,0:T(8,128)S(1)}, u32[]{:S(2)}, u32[]{:S(2)}) %collective-permute-start.68) | collective-permute-done | bytes 139296 | tf_op jit(solution)/shard_map/ppermute | solution.py:29
  154.5 2.9 %fusion = f32[128,2048]{1,0:T(8,128)S(1)} fusion(bf16[2048,2048]{1,0:T(8,128)(2,1)S(1)} %copy-done, f32[128,2048]{1,0:T(8,128)S(1)} %constant_dynamic-update-slice_fusion.112), kind=kOutput, calls=%fused_computation.8 | convolution fusion | flops 1074003968 | bytes 10485760 | tf_op jit(solution)/shard_map/dot_general | solution.py:17
  158.4 1.7 collective-permute-start.72
  160.1 1.9 %collective-permute-done.70 = f32[8,2176]{1,0:T(8,128)S(1)} collective-permute-done((f32[8,2176]{1,0:T(8,128)S(1)}, f32[8,2176]{1,0:T(8,128)S(1)}, u32[]{:S(2)}, u32[]{:S(2)}) %collective-permute-start.70) | collective-permute-done | bytes 69664 | tf_op jit(solution)/shard_map/ppermute | solution.py:29
  163.2 1.8 %collective-permute-done.72 = f32[8,2176]{1,0:T(8,128)S(1)} collective-permute-done((f32[8,2176]{1,0:T(8,128)S(1)}, f32[8,2176]{1,0:T(8,128)S(1)}, u32[]{:S(2)}, u32[]{:S(2)}) %collective-permute-start.72) | collective-permute-done | bytes 69664 | tf_op jit(solution)/shard_map/ppermute | solution.py:29
  165.7 2.1 %collective-permute-done.71 = f32[8,2176]{1,0:T(8,128)S(1)} collective-permute-done((f32[8,2176]{1,0:T(8,128)S(1)}, f32[8,2176]{1,0:T(8,128)S(1)}, u32[]{:S(2)}, u32[]{:S(2)}) %collective-permute-start.71) | collective-permute-done | bytes 69664 | tf_op jit(solution)/shard_map/ppermute | solution.py:29
  167.8 1.6 collective-permute-done.73
  (387 shorter events, 87.9 us)
Async XLA Ops:
  8.0 6.3 %collective-permute-start.2 = (f32[8,2176]{1,0:T(8,128)S(1)}, f32[8,2176]{1,0:T(8,128)S(1)}, u32[]{:S(2)}, u32[]{:S(2)}) collective-permute-start(f32[8,2176]{1,0:T(8,128)S(1)} %fusion.132), channel_id=1, source_target_pairs={{0,16},{4,20},{8,24},{12,28},{16,0},{20,4},{24,8},{28,12},{1,17},{... | collective-permute-start | bytes 208904 | tf_op jit(solution)/shard_map/ppermute | solution.py:29
  10.9 5.8 %collective-permute-start.3 = (f32[8,2176]{1,0:T(8,128)S(1)}, f32[8,2176]{1,0:T(8,128)S(1)}, u32[]{:S(2)}, u32[]{:S(2)}) collective-permute-start(f32[8,2176]{1,0:T(8,128)S(1)} %fusion.132), channel_id=1, source_target_pairs={{0,24},{4,28},{8,16},{12,20},{16,8},{20,12},{24,0},{28,4},{1,25},{... | collective-permute-start | bytes 208904 | tf_op jit(solution)/shard_map/ppermute | solution.py:29
  22.1 6.2 %collective-permute-start.6 = (f32[8,2176]{1,0:T(8,128)S(1)}, f32[8,2176]{1,0:T(8,128)S(1)}, u32[]{:S(2)}, u32[]{:S(2)}) collective-permute-start(f32[8,2176]{1,0:T(8,128)S(1)} %select_maximum_fusion.5), channel_id=1, source_target_pairs={{0,3},{1,2},{2,1},{3,0},{4,7},{5,6},{6,5},{7,4},{8,11},{9,10},{10,... | collective-permute-start | bytes 208904 | tf_op jit(solution)/shard_map/ppermute | solution.py:29
  41.3 7.2 %collective-permute-start.12 = (f32[8,2176]{1,0:T(8,128)S(1)}, f32[8,2176]{1,0:T(8,128)S(1)}, u32[]{:S(2)}, u32[]{:S(2)}) collective-permute-start(f32[8,2176]{1,0:T(8,128)S(1)} %select_maximum_fusion.3), channel_id=1, source_target_pairs={{0,2},{1,3},{2,0},{3,1},{4,6},{5,7},{6,4},{7,5},{8,10},{9,11},{10,... | collective-permute-start | bytes 208904 | tf_op jit(solution)/shard_map/ppermute | solution.py:29
  43.5 6.2 %collective-permute-start.13 = (f32[8,2176]{1,0:T(8,128)S(1)}, f32[8,2176]{1,0:T(8,128)S(1)}, u32[]{:S(2)}, u32[]{:S(2)}) collective-permute-start(f32[8,2176]{1,0:T(8,128)S(1)} %select_maximum_fusion.3), channel_id=1, source_target_pairs={{0,3},{1,2},{2,1},{3,0},{4,7},{5,6},{6,5},{7,4},{8,11},{9,10},{10,... | collective-permute-start | bytes 208904 | tf_op jit(solution)/shard_map/ppermute | solution.py:29
  55.0 6.6 %collective-permute-start.27 = (f32[16,2176]{1,0:T(8,128)S(1)}, f32[16,2176]{1,0:T(8,128)S(1)}, u32[]{:S(2)}, u32[]{:S(2)}) collective-permute-start(f32[16,2176]{1,0:T(8,128)S(1)} %get-tuple-element.24), channel_id=1, source_target_pairs={{0,16},{4,20},{8,24},{12,28},{16,0},{20,4},{24,8},{28,12},{1,17},{... | collective-permute-start | bytes 417800 | tf_op jit(solution)/shard_map/ppermute | solution.py:29
  56.4 6.5 %collective-permute-start.23 = (f32[16,2176]{1,0:T(8,128)S(1)}, f32[16,2176]{1,0:T(8,128)S(1)}, u32[]{:S(2)}, u32[]{:S(2)}) collective-permute-start(f32[16,2176]{1,0:T(8,128)S(1)} %get-tuple-element.25), channel_id=1, source_target_pairs={{0,8},{4,12},{8,0},{12,4},{16,24},{20,28},{24,16},{28,20},{1,9},{5... | collective-permute-start | bytes 417800 | tf_op jit(solution)/shard_map/ppermute | solution.py:29
  57.4 6.9 %collective-permute-start.19 = (f32[16,2176]{1,0:T(8,128)S(1)}, f32[16,2176]{1,0:T(8,128)S(1)}, u32[]{:S(2)}, u32[]{:S(2)}) collective-permute-start(f32[16,2176]{1,0:T(8,128)S(1)} %get-tuple-element.26), channel_id=1, source_target_pairs={{0,16},{4,20},{8,24},{12,28},{16,0},{20,4},{24,8},{28,12},{1,17},{... | collective-permute-start | bytes 417800 | tf_op jit(solution)/shard_map/ppermute | solution.py:29
  58.1 7.8 %collective-permute-start.15 = (f32[16,2176]{1,0:T(8,128)S(1)}, f32[16,2176]{1,0:T(8,128)S(1)}, u32[]{:S(2)}, u32[]{:S(2)}) collective-permute-start(f32[16,2176]{1,0:T(8,128)S(1)} %get-tuple-element.27), channel_id=1, source_target_pairs={{0,8},{4,12},{8,0},{12,4},{16,24},{20,28},{24,16},{28,20},{1,9},{5... | collective-permute-start | bytes 417800 | tf_op jit(solution)/shard_map/ppermute | solution.py:29
  61.6 7.3 %collective-permute-start.28 = (f32[16,2176]{1,0:T(8,128)S(1)}, f32[16,2176]{1,0:T(8,128)S(1)}, u32[]{:S(2)}, u32[]{:S(2)}) collective-permute-start(f32[16,2176]{1,0:T(8,128)S(1)} %add.293), channel_id=1, source_target_pairs={{0,8},{4,12},{8,0},{12,4},{16,24},{20,28},{24,16},{28,20},{1,9},{5... | collective-permute-start | bytes 417800 | tf_op jit(solution)/shard_map/ppermute | solution.py:29
  62.9 7.1 %collective-permute-start.24 = (f32[16,2176]{1,0:T(8,128)S(1)}, f32[16,2176]{1,0:T(8,128)S(1)}, u32[]{:S(2)}, u32[]{:S(2)}) collective-permute-start(f32[16,2176]{1,0:T(8,128)S(1)} %add.290), channel_id=1, source_target_pairs={{0,16},{4,20},{8,24},{12,28},{16,0},{20,4},{24,8},{28,12},{1,17},{... | collective-permute-start | bytes 417800 | tf_op jit(solution)/shard_map/ppermute | solution.py:29
  64.3 7.3 %collective-permute-start.20 = (f32[16,2176]{1,0:T(8,128)S(1)}, f32[16,2176]{1,0:T(8,128)S(1)}, u32[]{:S(2)}, u32[]{:S(2)}) collective-permute-start(f32[16,2176]{1,0:T(8,128)S(1)} %add.287), channel_id=1, source_target_pairs={{0,8},{4,12},{8,0},{12,4},{16,24},{20,28},{24,16},{28,20},{1,9},{5... | collective-permute-start | bytes 417800 | tf_op jit(solution)/shard_map/ppermute | solution.py:29
  65.9 6.5 %collective-permute-start.16 = (f32[16,2176]{1,0:T(8,128)S(1)}, f32[16,2176]{1,0:T(8,128)S(1)}, u32[]{:S(2)}, u32[]{:S(2)}) collective-permute-start(f32[16,2176]{1,0:T(8,128)S(1)} %add.284), channel_id=1, source_target_pairs={{0,16},{4,20},{8,24},{12,28},{16,0},{20,4},{24,8},{28,12},{1,17},{... | collective-permute-start | bytes 417800 | tf_op jit(solution)/shard_map/ppermute | solution.py:29
  79.1 6.6 %collective-permute-start.32 = (f32[8,2176]{1,0:T(8,128)S(1)}, f32[8,2176]{1,0:T(8,128)S(1)}, u32[]{:S(2)}, u32[]{:S(2)}) collective-permute-start(f32[8,2176]{1,0:T(8,128)S(1)} %get-tuple-element.60), channel_id=1, source_target_pairs={{0,2},{1,3},{2,0},{3,1},{4,6},{5,7},{6,4},{7,5},{8,10},{9,11},{10,... | collective-permute-start | bytes 208904 | tf_op jit(solution)/shard_map/ppermute | solution.py:29
  94.9 6.6 %collective-permute-start.47 = (f32[16,2176]{1,0:T(8,128)S(1)}, f32[16,2176]{1,0:T(8,128)S(1)}, u32[]{:S(2)}, u32[]{:S(2)}) collective-permute-start(f32[16,2176]{1,0:T(8,128)S(1)} %get-tuple-element.16), channel_id=1, source_target_pairs={{0,16},{4,20},{8,24},{12,28},{16,0},{20,4},{24,8},{28,12},{1,17},{... | collective-permute-start | bytes 417800 | tf_op jit(solution)/shard_map/ppermute | solution.py:29
  95.7 6.9 %collective-permute-start.43 = (f32[16,2176]{1,0:T(8,128)S(1)}, f32[16,2176]{1,0:T(8,128)S(1)}, u32[]{:S(2)}, u32[]{:S(2)}) collective-permute-start(f32[16,2176]{1,0:T(8,128)S(1)} %get-tuple-element.17), channel_id=1, source_target_pairs={{0,8},{4,12},{8,0},{12,4},{16,24},{20,28},{24,16},{28,20},{1,9},{5... | collective-permute-start | bytes 417800 | tf_op jit(solution)/shard_map/ppermute | solution.py:29
  96.6 7.3 %collective-permute-start.39 = (f32[16,2176]{1,0:T(8,128)S(1)}, f32[16,2176]{1,0:T(8,128)S(1)}, u32[]{:S(2)}, u32[]{:S(2)}) collective-permute-start(f32[16,2176]{1,0:T(8,128)S(1)} %get-tuple-element.18), channel_id=1, source_target_pairs={{0,16},{4,20},{8,24},{12,28},{16,0},{20,4},{24,8},{28,12},{1,17},{... | collective-permute-start | bytes 417800 | tf_op jit(solution)/shard_map/ppermute | solution.py:29
  97.9 7.3 %collective-permute-start.35 = (f32[16,2176]{1,0:T(8,128)S(1)}, f32[16,2176]{1,0:T(8,128)S(1)}, u32[]{:S(2)}, u32[]{:S(2)}) collective-permute-start(f32[16,2176]{1,0:T(8,128)S(1)} %get-tuple-element.19), channel_id=1, source_target_pairs={{0,8},{4,12},{8,0},{12,4},{16,24},{20,28},{24,16},{28,20},{1,9},{5... | collective-permute-start | bytes 417800 | tf_op jit(solution)/shard_map/ppermute | solution.py:29
  101.5 6.7 %collective-permute-start.48 = (f32[16,2176]{1,0:T(8,128)S(1)}, f32[16,2176]{1,0:T(8,128)S(1)}, u32[]{:S(2)}, u32[]{:S(2)}) collective-permute-start(f32[16,2176]{1,0:T(8,128)S(1)} %add.316), channel_id=1, source_target_pairs={{0,8},{4,12},{8,0},{12,4},{16,24},{20,28},{24,16},{28,20},{1,9},{5... | collective-permute-start | bytes 417800 | tf_op jit(solution)/shard_map/ppermute | solution.py:29
  102.6 6.6 %collective-permute-start.44 = (f32[16,2176]{1,0:T(8,128)S(1)}, f32[16,2176]{1,0:T(8,128)S(1)}, u32[]{:S(2)}, u32[]{:S(2)}) collective-permute-start(f32[16,2176]{1,0:T(8,128)S(1)} %add.313), channel_id=1, source_target_pairs={{0,16},{4,20},{8,24},{12,28},{16,0},{20,4},{24,8},{28,12},{1,17},{... | collective-permute-start | bytes 417800 | tf_op jit(solution)/shard_map/ppermute | solution.py:29
  103.9 6.7 %collective-permute-start.40 = (f32[16,2176]{1,0:T(8,128)S(1)}, f32[16,2176]{1,0:T(8,128)S(1)}, u32[]{:S(2)}, u32[]{:S(2)}) collective-permute-start(f32[16,2176]{1,0:T(8,128)S(1)} %add.310), channel_id=1, source_target_pairs={{0,8},{4,12},{8,0},{12,4},{16,24},{20,28},{24,16},{28,20},{1,9},{5... | collective-permute-start | bytes 417800 | tf_op jit(solution)/shard_map/ppermute | solution.py:29
  105.2 6.3 %collective-permute-start.36 = (f32[16,2176]{1,0:T(8,128)S(1)}, f32[16,2176]{1,0:T(8,128)S(1)}, u32[]{:S(2)}, u32[]{:S(2)}) collective-permute-start(f32[16,2176]{1,0:T(8,128)S(1)} %add.307), channel_id=1, source_target_pairs={{0,16},{4,20},{8,24},{12,28},{16,0},{20,4},{24,8},{28,12},{1,17},{... | collective-permute-start | bytes 417800 | tf_op jit(solution)/shard_map/ppermute | solution.py:29
  117.8 6.8 %collective-permute-start.52 = (f32[8,2176]{1,0:T(8,128)S(1)}, f32[8,2176]{1,0:T(8,128)S(1)}, u32[]{:S(2)}, u32[]{:S(2)}) collective-permute-start(f32[8,2176]{1,0:T(8,128)S(1)} %get-tuple-element.58), channel_id=1, source_target_pairs={{0,2},{1,3},{2,0},{3,1},{4,6},{5,7},{6,4},{7,5},{8,10},{9,11},{10,... | collective-permute-start | bytes 208904 | tf_op jit(solution)/shard_map/ppermute | solution.py:29
  134.4 6.6 %collective-permute-start.67 = (f32[16,2176]{1,0:T(8,128)S(1)}, f32[16,2176]{1,0:T(8,128)S(1)}, u32[]{:S(2)}, u32[]{:S(2)}) collective-permute-start(f32[16,2176]{1,0:T(8,128)S(1)} %get-tuple-element.8), channel_id=1, source_target_pairs={{0,16},{4,20},{8,24},{12,28},{16,0},{20,4},{24,8},{28,12},{1,17},{... | collective-permute-start | bytes 417800 | tf_op jit(solution)/shard_map/ppermute | solution.py:29
  135.8 6.5 %collective-permute-start.63 = (f32[16,2176]{1,0:T(8,128)S(1)}, f32[16,2176]{1,0:T(8,128)S(1)}, u32[]{:S(2)}, u32[]{:S(2)}) collective-permute-start(f32[16,2176]{1,0:T(8,128)S(1)} %get-tuple-element.9), channel_id=1, source_target_pairs={{0,8},{4,12},{8,0},{12,4},{16,24},{20,28},{24,16},{28,20},{1,9},{5... | collective-permute-start | bytes 417800 | tf_op jit(solution)/shard_map/ppermute | solution.py:29
  136.7 6.8 %collective-permute-start.59 = (f32[16,2176]{1,0:T(8,128)S(1)}, f32[16,2176]{1,0:T(8,128)S(1)}, u32[]{:S(2)}, u32[]{:S(2)}) collective-permute-start(f32[16,2176]{1,0:T(8,128)S(1)} %get-tuple-element.10), channel_id=1, source_target_pairs={{0,16},{4,20},{8,24},{12,28},{16,0},{20,4},{24,8},{28,12},{1,17},{... | collective-permute-start | bytes 417800 | tf_op jit(solution)/shard_map/ppermute | solution.py:29
  137.2 8.1 %collective-permute-start.55 = (f32[16,2176]{1,0:T(8,128)S(1)}, f32[16,2176]{1,0:T(8,128)S(1)}, u32[]{:S(2)}, u32[]{:S(2)}) collective-permute-start(f32[16,2176]{1,0:T(8,128)S(1)} %get-tuple-element.11), channel_id=1, source_target_pairs={{0,8},{4,12},{8,0},{12,4},{16,24},{20,28},{24,16},{28,20},{1,9},{5... | collective-permute-start | bytes 417800 | tf_op jit(solution)/shard_map/ppermute | solution.py:29
  141.0 7.3 %collective-permute-start.68 = (f32[16,2176]{1,0:T(8,128)S(1)}, f32[16,2176]{1,0:T(8,128)S(1)}, u32[]{:S(2)}, u32[]{:S(2)}) collective-permute-start(f32[16,2176]{1,0:T(8,128)S(1)} %add.339), channel_id=1, source_target_pairs={{0,8},{4,12},{8,0},{12,4},{16,24},{20,28},{24,16},{28,20},{1,9},{5... | collective-permute-start | bytes 417800 | tf_op jit(solution)/shard_map/ppermute | solution.py:29
  142.4 6.9 %collective-permute-start.64 = (f32[16,2176]{1,0:T(8,128)S(1)}, f32[16,2176]{1,0:T(8,128)S(1)}, u32[]{:S(2)}, u32[]{:S(2)}) collective-permute-start(f32[16,2176]{1,0:T(8,128)S(1)} %add.336), channel_id=1, source_target_pairs={{0,16},{4,20},{8,24},{12,28},{16,0},{20,4},{24,8},{28,12},{1,17},{... | collective-permute-start | bytes 417800 | tf_op jit(solution)/shard_map/ppermute | solution.py:29
  143.5 7.3 %collective-permute-start.60 = (f32[16,2176]{1,0:T(8,128)S(1)}, f32[16,2176]{1,0:T(8,128)S(1)}, u32[]{:S(2)}, u32[]{:S(2)}) collective-permute-start(f32[16,2176]{1,0:T(8,128)S(1)} %add.333), channel_id=1, source_target_pairs={{0,8},{4,12},{8,0},{12,4},{16,24},{20,28},{24,16},{28,20},{1,9},{5... | collective-permute-start | bytes 417800 | tf_op jit(solution)/shard_map/ppermute | solution.py:29
  145.3 6.3 %collective-permute-start.56 = (f32[16,2176]{1,0:T(8,128)S(1)}, f32[16,2176]{1,0:T(8,128)S(1)}, u32[]{:S(2)}, u32[]{:S(2)}) collective-permute-start(f32[16,2176]{1,0:T(8,128)S(1)} %add.330), channel_id=1, source_target_pairs={{0,16},{4,20},{8,24},{12,28},{16,0},{20,4},{24,8},{28,12},{1,17},{... | collective-permute-start | bytes 417800 | tf_op jit(solution)/shard_map/ppermute | solution.py:29
  158.4 6.6 %collective-permute-start.72 = (f32[8,2176]{1,0:T(8,128)S(1)}, f32[8,2176]{1,0:T(8,128)S(1)}, u32[]{:S(2)}, u32[]{:S(2)}) collective-permute-start(f32[8,2176]{1,0:T(8,128)S(1)} %get-tuple-element.56), channel_id=1, source_target_pairs={{0,2},{1,3},{2,0},{3,1},{4,6},{5,7},{6,4},{7,5},{8,10},{9,11},{10,... | collective-permute-start | bytes 208904 | tf_op jit(solution)/shard_map/ppermute | solution.py:29
  (50 other events, 278.2 us)
